TPU v7x, 32 devices: a whole 2x2x4 slice. The times are simulated.
32 devices in a mesh: zone: 4 (over y, x), slab: 8 (over z, core).
Axes of the slice: x: 2, y: 2, z: 4, core: 2. Of those that a mesh axis runs over, the one named last changes fastest.
Arguments:
- tracers: float32 [4, 4, 2048, 2048], P('zone', None, 'slab'), may hold values from -6 to 6
- velocity: float32 [4, 2, 2048, 2048], P('zone', None, 'slab'), may hold values from -0.2 to 0.2
- diffusivity: float32 [4], replicated, may hold values from 0.02 to 0.12
- owner_dev: int32 [512, 2], P('slab'), may hold values from 0 to 23, all different within a row; in each aligned block of 64 rows (0 to 63, 64 to 127, ...) at most 7 rows name the same one
- owner_seg: int32 [512, 2], P('slab'), may hold values from 0 to 63
- intersection: float32 [512, 2], P('slab'), may hold values from 0.2 to 1
Outputs:
- updated: float32 [4, 4, 2048, 2048], P('zone', None, 'slab')
Inputs may be any that keep to these rules, and one draw needn't show every extreme that they name: owner_dev names workpiece slab zone * 8 + slab; the 2 entries of a row differ; the rows of one pin slab name one workpiece slab at most 7 times, and some name one exactly 7 times.
All inputs are finite; a program needn't handle non-finite values.
Results may differ from a plain program's by a relative error of at most 0.00007.
Values sent between devices are 32-bit elements; how exact they have to be, the bound alone decides.
No kernel may reach another device: no remote copies, remote signals or barrier semaphores. Data moves between devices by JAX's collectives and lax.ppermute only.
A program may use at most 128 MiB of HBM per device.

v0:
```python
import jax
import jax.numpy as jnp
from jax import lax
from jax.sharding import PartitionSpec as P

SEG = 32


COUPLE = 0.5


def extended(block, sides, width):
    for axis, dim in sides:
        count = lax.axis_size(axis)
        forward = [(i, i + 1) for i in range(count - 1)]
        backward = [(target, source) for source, target in forward]
        low = lax.ppermute(
            lax.slice_in_dim(block, block.shape[dim] - width, None, axis=dim), axis, forward
        )
        high = lax.ppermute(lax.slice_in_dim(block, 0, width, axis=dim), axis, backward)
        block = jnp.concatenate([low, block, high], axis=dim)
    return block


def from_root(block, axis, owner):
    block = jnp.where(lax.axis_index(axis) == owner, block, jnp.zeros_like(block))
    return lax.psum(block, axis)


def advance(center, upper_row, lower_row, velocity, diffusivity):
    left_cells = jnp.roll(center, 1, axis=3)
    right_cells = jnp.roll(center, -1, axis=3)
    along_rows = velocity[:, 0][:, None]
    along_cols = velocity[:, 1][:, None]
    transport = jnp.maximum(along_rows, 0.0) * (center - upper_row) + jnp.minimum(
        along_rows, 0.0
    ) * (lower_row - center)
    transport = (
        transport
        + jnp.maximum(along_cols, 0.0) * (center - left_cells)
        + jnp.minimum(along_cols, 0.0) * (right_cells - center)
    )
    laplace = upper_row + lower_row + left_cells + right_cells - 4.0 * center
    return center + diffusivity[None, :, None, None] * laplace - transport


def shards(tracers, velocity, diffusivity, owner_dev, owner_seg, intersection):
    zone_count = lax.axis_size("zone")
    slab_count = lax.axis_size("slab")
    zone_index = lax.axis_index("zone")
    padded = extended(tracers, (("slab", 2),), 1)
    stepped = advance(
        padded[:, :, 1:-1], padded[:, :, :-2], padded[:, :, 2:], velocity, diffusivity
    )
    tracer_count = tracers.shape[1]
    row_count = tracers.shape[2]
    col_count = tracers.shape[3]
    seg_count = col_count // SEG
    payload = tracer_count * SEG
    own_face = (
        tracers[0, :, row_count - 1, :]
        .reshape(tracer_count, seg_count, SEG)
        .transpose(1, 0, 2)
        .reshape(seg_count, payload)
    )
    pin_face = from_root(own_face, "zone", zone_count - 1)
    fanout = owner_dev.shape[1]
    item_count = owner_dev.shape[0] * fanout
    target_dev = owner_dev.reshape(item_count)
    target_seg = owner_seg.reshape(item_count)
    weight = intersection.reshape(item_count)
    in_zone = target_dev // slab_count == zone_index
    target_slab = target_dev % slab_count
    pin_values = jnp.repeat(pin_face, fanout, axis=0)
    highest = lax.Precision.HIGHEST
    zone_faces = lax.all_gather(own_face, "slab", axis=0, tiled=True)
    slot_ids = jnp.arange(slab_count * seg_count, dtype=jnp.int32)
    picker = (
        ((target_slab * seg_count + target_seg)[:, None] == slot_ids[None, :]) & in_zone[:, None]
    ).astype(jnp.float32)
    owner_values = jnp.dot(picker, zone_faces, precision=highest)
    item_flux = jnp.where(in_zone, weight, 0.0)[:, None] * (pin_values - owner_values)
    inflow = lax.psum_scatter(
        jnp.dot(picker.T, item_flux, precision=highest), "slab", scatter_dimension=0, tiled=True
    )
    pin_part = jnp.sum(item_flux.reshape(seg_count, fanout, payload), axis=1)
    pin_total = lax.psum(pin_part, "zone")
    is_pin = zone_index == zone_count - 1
    coupling = COUPLE * inflow - jnp.where(is_pin, COUPLE * pin_total, 0.0)
    coupling = (
        coupling.reshape(seg_count, tracer_count, SEG)
        .transpose(1, 0, 2)
        .reshape(tracer_count, col_count)
    )
    return stepped.at[0, :, row_count - 1, :].add(coupling)


def solution(mesh):
    placed = (
        P("zone", None, "slab", None),
        P("zone", None, "slab", None),
        P(),
        P("slab", None),
        P("slab", None),
        P("slab", None),
    )
    return jax.shard_map(
        shards, mesh=mesh, in_specs=placed, out_specs=P("zone", None, "slab", None), check_vma=False
    )
```

profile of v0, /device:TPU:0, one launch (start us, length us, event | category | flops | bytes accessed | tf_op | source)
XLA Modules:
  0.0 115.7 jit_solution(10784930607515676139)
XLA Ops:
  6.5 0.0 reduce-scatter.2.cloned.1.call-start
  6.5 1.2 slice_reduce_fusion
  7.7 0.1 reshape_squeeze.3
  7.8 0.1 copy.60
  7.9 0.1 copy.61
  7.9 15.9 %all_gather.3 = f32[512,128]{1,0:T(8,128)S(1)} all-gather(f32[64,128]{1,0:T(8,128)S(1)} %copy.61), channel_id=1, replica_groups=mesh['zone'=4,'slab'=8] {'slab'}, dimensions={0}, use_global_device_ids=true | all-gather | bytes 294912 | tf_op jit(solution)/shard_map/all_gather | solution.py:76
  23.9 16.3 %psum.14 = f32[64,128]{1,0:T(8,128)S(1)} all-reduce(f32[64,128]{1,0:T(8,128)S(1)} %broadcast_select_fusion.1), channel_id=1, replica_groups=mesh['zone'=4,'slab'=8] {'zone'}, use_global_device_ids=true, to_apply=%region_1.2 | all-reduce | flops 8192 | bytes 65536 | tf_op jit(solution)/shard_map/psum | solution.py:27
  40.1 0.8 copy.57
  40.9 0.1 reshape.148
  41.1 0.8 copy.59
  41.8 0.1 reshape.150
  42.0 0.8 copy.58
  42.7 0.1 reshape.149
  42.9 0.3 fusion.14
  43.3 1.2 %fusion.16 = f32[512,128]{1,0:T(8,128)} fusion(f32[128,128]{1,0:T(8,128)S(1)} %fusion.14, s32[128]{0:T(128)S(1)} %fusion.24, pred[128]{0:T(512)(128)(4,1)S(1)} %get-tuple-element.18), kind=kOutput, calls=%fused_computation.26 | convolution fusion | flops 100794368 | bytes 328320 | tf_op jit(solution)/shard_map/dot_general | solution.py:84
  44.4 0.0 reduce-scatter.2.cloned.1.call-update
  44.5 1.3 %collective-permute-start = (f32[1,4,1,2048]{3,2,1,0:T(1,128)S(1)}, f32[1,4,1,2048]{3,2,1,0:T(1,128)S(1)}, u32[]{:S(2)}, u32[]{:S(2)}) collective-permute-start(f32[1,4,1,2048]{3,2,1,0:T(1,128)S(1)} %get-tuple-element.21), channel_id=1, source_target_pairs={{0,1},{1,2},{2,3},{3,4},{4,5},{5,6},{6,7},{8,9},{9,10},{10,11},{11... | collective-permute-start | bytes 98312 | tf_op jit(solution)/shard_map/ppermute | solution.py:17
  45.8 0.0 copy-start
  45.8 1.6 %collective-permute-start.1 = (f32[1,4,1,2048]{3,2,1,0:T(1,128)S(1)}, f32[1,4,1,2048]{3,2,1,0:T(1,128)S(1)}, u32[]{:S(2)}, u32[]{:S(2)}) collective-permute-start(f32[1,4,1,2048]{3,2,1,0:T(1,128)S(1)} %get-tuple-element.20), channel_id=1, source_target_pairs={{1,0},{2,1},{3,2},{4,3},{5,4},{6,5},{7,6},{9,8},{10,9},{11,10},{12... | collective-permute-start | bytes 98312 | tf_op jit(solution)/shard_map/ppermute | solution.py:20
  47.3 13.3 %fusion.28 = (f32[1,4,256,2047]{3,2,1,0:T(8,128)}, f32[1,4,256,2047]{3,2,1,0:T(8,128)}) fusion(f32[1,4,256,2048]{3,2,1,0:T(8,128)} %param.8), kind=kLoop, calls=%fused_computation.47 | loop fusion | bytes 33538048 | tf_op jit(solution)/shard_map/jit(_roll_static)/slice | solution.py:31
  60.6 0.0 copy-start.2
  60.6 0.0 copy-start.1
  60.6 1.4 %fusion.27 = (f32[1,4,256,1]{3,2,1,0:T(8,128)S(1)}, f32[1,4,256,1]{3,2,1,0:T(8,128)S(1)}) fusion(f32[1,4,256,2048]{3,2,1,0:T(8,128)} %param.8), kind=kLoop, calls=%fused_computation.46 | loop fusion | bytes 16384 | tf_op jit(solution)/shard_map/jit(_roll_static)/slice | solution.py:31
  62.1 0.0 copy-done
  62.1 2.9 %maximum_bitcast_fusion.1 = (f32[256,2048]{1,0:T(8,128)S(1)}, f32[256,2048]{1,0:T(8,128)}, f32[256,2048]{1,0:T(8,128)}, f32[256,2048]{1,0:T(8,128)}) fusion(f32[1,2,256,2048]{3,2,1,0:T(8,128)S(1)} %copy-done), kind=kLoop, calls=%fused_computation.21 | loop fusion | flops 2097152 | bytes 12582912 | tf_op jit(solution)/shard_map/mul | solution.py:35
  65.0 0.6 fusion.29
  65.6 0.0 copy-done.2
  65.6 2.0 %and_reduce_fusion = pred[]{:T(512)} fusion(s32[4]{0:T(128)S(1)} %copy-done.2, s32[1]{0:T(128)} %constant.60.clone.1, s32[1]{0:T(128)} %get-tuple-element.31, s32[1]{0:T(128)} %get-tuple-element.30), kind=kLoop, calls=%fused_computation.36 | loop fusion | flops 27 | bytes 29 | tf_op jit(solution)/shard_map/reduce.1
  67.6 0.1 reduce_sum.9
  67.7 14.3 %psum.15 = f32[64,128]{1,0:T(8,128)S(1)} all-reduce(f32[64,128]{1,0:T(8,128)S(1)} %reduce_sum.9), channel_id=1, replica_groups=mesh['zone'=4,'slab'=8] {'zone'}, use_global_device_ids=true, to_apply=%region_4.5 | all-reduce | flops 8192 | bytes 65536 | tf_op jit(solution)/shard_map/psum | solution.py:87
  82.0 0.0 collective-permute-done
  82.0 0.0 collective-permute-done.1
  82.0 0.0 copy-done.1
  82.0 21.2 %fusion.6 = f32[1,4,256,2048]{3,2,1,0:T(8,128)} fusion(f32[1,4,256,2048]{3,2,1,0:T(8,128)} %param.8, f32[1,4,1,2048]{3,2,1,0:T(1,128)S(1)} %collective-permute-done.1, f32[1,4,1,2048]{3,2,1,0:T(1,128)S(1)} %collective-permute-done, f32[1,4,256,1]{3,2,1,0:T(8,128)S(1)} %get-tuple-element.23, f32[1,4,256,2047]{3,2,1,0:T(8,128)} %get-tuple-element.25, ...), kind=kLoop, calls=%fused_computation.7 | loop fusion | flops 48234496 | bytes 42008592 | tf_op jit(solution)/shard_map/sub | solution.py:44
  103.2 0.0 reduce-scatter.2.cloned.1.call-done
  103.2 0.8 select_subtract_fusion
  103.9 0.1 copy.63
  104.0 0.1 copy.64
  104.1 0.1 reshape.156
  104.3 2.2 %broadcast_select_fusion = f32[1,4,1,2048]{3,2,1,0:T(1,128)S(1)} fusion(pred[]{:T(512)} %and_reduce_fusion, f32[1,4,1,2048]{3,2,1,0:T(1,128)S(1)} %reshape.156, f32[1,4,256,2048]{3,2,1,0:T(8,128)} %fusion.6, s32[]{:T(128)} %bitcast.4), kind=kLoop, calls=%fused_computation.31 | loop fusion | flops 16384 | bytes 98309 | tf_op jit(solution)/shard_map/select.1
  106.5 2.4 %scatter-add.4 = f32[1,4,256,2048]{3,2,1,0:T(8,128)} dynamic-update-slice(f32[1,4,256,2048]{3,2,1,0:T(8,128)} %fusion.6, f32[1,4,1,2048]{3,2,1,0:T(1,128)S(1)} %broadcast_select_fusion, s32[]{:T(128)} %constant.58.clone.1, s32[]{:T(128)} %constant.58.clone.1, s32[]{:T(128)} %bitcast.4, s32[]{:T(128)} %constant.58.clone.1) | dynamic-update-slice | bytes 65540 | tf_op jit(solution)/shard_map/scatter-add | solution.py:95
  (5 shorter events, 0.1 us)
Async XLA Ops:
  6.5 96.6 %reduce-scatter.2.cloned.1.call-start = ((), (), s32[]{:S(2)}) async-start(), calls=%async_computation.1 | async-start | bytes 294912 | tf_op jit(solution)/shard_map/reduce_scatter | solution.py:83
  44.5 37.5 %collective-permute-start = (f32[1,4,1,2048]{3,2,1,0:T(1,128)S(1)}, f32[1,4,1,2048]{3,2,1,0:T(1,128)S(1)}, u32[]{:S(2)}, u32[]{:S(2)}) collective-permute-start(f32[1,4,1,2048]{3,2,1,0:T(1,128)S(1)} %get-tuple-element.21), channel_id=1, source_target_pairs={{0,1},{1,2},{2,3},{3,4},{4,5},{5,6},{6,7},{8,9},{9,10},{10,11},{11... | collective-permute-start | bytes 98312 | tf_op jit(solution)/shard_map/ppermute | solution.py:17
  45.8 16.3 %copy-start = (f32[1,2,256,2048]{3,2,1,0:T(8,128)S(1)}, f32[1,2,256,2048]{3,2,1,0:T(8,128)}, u32[]{:S(2)}) copy-start(f32[1,2,256,2048]{3,2,1,0:T(8,128)} %param.9) | copy-start | bytes 12582916
  45.8 36.2 %collective-permute-start.1 = (f32[1,4,1,2048]{3,2,1,0:T(1,128)S(1)}, f32[1,4,1,2048]{3,2,1,0:T(1,128)S(1)}, u32[]{:S(2)}, u32[]{:S(2)}) collective-permute-start(f32[1,4,1,2048]{3,2,1,0:T(1,128)S(1)} %get-tuple-element.20), channel_id=1, source_target_pairs={{1,0},{2,1},{3,2},{4,3},{5,4},{6,5},{7,6},{9,8},{10,9},{11,10},{12... | collective-permute-start | bytes 98312 | tf_op jit(solution)/shard_map/ppermute | solution.py:20
  60.6 5.0 %copy-start.2 = (s32[4]{0:T(128)S(1)}, s32[4]{0:T(128)}, u32[]{:S(2)}) copy-start(s32[4]{0:T(128)} %constant.61.clone.1) | copy-start | bytes 52
  60.6 21.4 %copy-start.1 = (f32[4]{0:T(128)S(1)}, f32[4]{0:T(128)}, u32[]{:S(2)}) copy-start(f32[4]{0:T(128)} %param.10) | copy-start | bytes 52
Sparse Core Ops, SparseCore 0:
  44.6 29.7 reduce-scatter.1
where the time goes:
time: 118 us; the launch traced here: 116 us
  blocking collectives  46.5 us (39%)
  other arithmetic  29.2 us (25%)
  local copies, waits for them, and re-layouts  22.2 us (19%)
  between operations  13.5 us (11%)
  starting transfers between devices  2.85 us (2%)
  matrix products  1.48 us (1%)
    sub x1, other arithmetic, advance(): return center + diffusivity[None, :, None, None] * laplace - transport  21.2 us
    psum x1, blocking collectives, from_root(): return lax.psum(block, axis)  16.3 us
    all_gather x1, blocking collectives, shards(): zone_faces = lax.all_gather(own_face, 'slab', axis=0, tiled=True)  15.9 us
    slice x2, local copies, waits for them, and re-layouts, advance(): left_cells = jnp.roll(center, 1, axis=3)  14.7 us
    psum x1, blocking collectives, shards(): pin_total = lax.psum(pin_part, 'zone')  14.3 us
    another operation x3, other arithmetic  4.17 us
    mul x1, other arithmetic, advance(): jnp.maximum(along_rows, 0.0) * (center - upper_row)  2.92 us
    scatter-add x1, local copies, waits for them, and re-layouts, shards(): return stepped.at[0, :, row_count - 1, :].add(coupling)  2.4 us
  transfers between devices with their start and end apart: 3, of which 0 were waited for; matrix products, arithmetic and copies ran while one was open for 36% of the time, Pallas kernels for 0%

commit v1 on v0

v1 whole, which is shorter than its diff:
```python
import functools

import jax
import jax.numpy as jnp
from jax import lax
from jax.experimental import pallas as pl
from jax.experimental.pallas import tpu as pltpu
from jax.sharding import PartitionSpec as P

SEG = 32
LANES = 128
TILE = 8
COUPLE = 0.5
HIGHEST = lax.Precision.HIGHEST
VMEM = pl.BlockSpec(memory_space=pltpu.VMEM)
SMEM = pl.BlockSpec(memory_space=pltpu.SMEM)
ANY = pl.BlockSpec(memory_space=pl.ANY)


def permuted(segment, blocks):
    quarters = LANES // SEG
    return (segment % quarters) * blocks + segment // quarters


def lane_group(shape):
    return lax.broadcasted_iota(jnp.int32, shape, len(shape) - 1) // SEG


def to_face(rows):
    quarters = LANES // SEG
    out = []
    for u in range(quarters):
        face = None
        for t, row in enumerate(rows):
            moved = row if t == u else pltpu.roll(row, ((t - u) * SEG) % LANES, 1)
            face = moved if face is None else jnp.where(lane_group(row.shape) == t, moved, face)
        out.append(face)
    return out


def from_face(face, tracer_count):
    quarters = LANES // SEG
    blocks = face.shape[0] // quarters
    rows = []
    for t in range(tracer_count):
        row = None
        for u in range(quarters):
            part = face[u * blocks : (u + 1) * blocks]
            moved = part if t == u else pltpu.roll(part, ((u - t) * SEG) % LANES, 1)
            row = moved if row is None else jnp.where(lane_group(part.shape) == u, moved, row)
        rows.append(row)
    return rows


def pack_kernel(top_ref, bottom_ref, dev_ref, seg_ref, weight_ref, out_ref, first_ref, rows_ref):
    tracer_count, _, cols = bottom_ref.shape[1:]
    blocks = cols // LANES
    segs = dev_ref.shape[0]
    for t in range(tracer_count):
        first_ref[t : t + 1, :] = top_ref[0, t, 0:1, :]
        for c in range(blocks):
            rows_ref[t, c : c + 1, :] = bottom_ref[0, t, TILE - 1 : TILE, c * LANES : (c + 1) * LANES]
    face = to_face([rows_ref[t] for t in range(tracer_count)])
    lane = lax.broadcasted_iota(jnp.int32, (segs, LANES), 1)
    row = lax.broadcasted_iota(jnp.int32, (segs, LANES), 0)
    mine = lane % segs == permuted(row, blocks)
    target = dev_ref[...] * segs + permuted(seg_ref[...], blocks)
    target = target.astype(jnp.float32)
    weight = weight_ref[...]
    fanout = target.shape[1]

    def in_lanes(table):
        picked = table[:, 0:1]
        for k in range(1, fanout):
            picked = jnp.where(lane < k * segs, picked, table[:, k : k + 1])
        return jnp.sum(jnp.where(mine, picked, 0.0), axis=0, keepdims=True)

    targets, weights = in_lanes(target), in_lanes(weight)
    index = lax.broadcasted_iota(jnp.int32, (TILE, LANES), 0)
    tables = jnp.where(index == 0, targets, jnp.where(index == 1, weights, 0.0))
    for slab in range(out_ref.shape[0]):
        for u, part in enumerate(face):
            out_ref[slab, u * blocks : (u + 1) * blocks, :] = part
        out_ref[slab, segs : segs + TILE, :] = tables


def middle_kernel(gathered_ref, dev_ref, seg_ref, weight_ref, out_ref):
    slab_count = gathered_ref.shape[0]
    zone_count, segs, _ = out_ref.shape
    fanout = dev_ref.shape[1]
    quarters = LANES // SEG
    blocks = segs // quarters
    zone, slab = lax.axis_index("zone"), lax.axis_index("slab")
    out_ref[...] = jnp.zeros_like(out_ref)

    def reordered(ref):
        return jnp.concatenate([ref[pl.ds(u, blocks, stride=quarters), :] for u in range(quarters)], axis=0)

    weight = reordered(weight_ref)

    @pl.when(zone < zone_count - 1)
    def _():
        target = reordered(dev_ref) * segs + permuted(reordered(seg_ref), blocks)
        slots = lax.broadcasted_iota(jnp.int32, (segs, slab_count * segs), 1) + zone * (slab_count * segs)
        picker = jnp.zeros(slots.shape, jnp.float32)
        for k in range(fanout):
            picker = picker + jnp.where(target[:, k : k + 1] == slots, weight[:, k : k + 1], 0.0)
        faces = jnp.concatenate([gathered_ref[i, :segs, :] for i in range(slab_count)], axis=0)
        out_ref[zone_count - 1] = jnp.dot(picker, faces, precision=HIGHEST, preferred_element_type=jnp.float32)
        own = lax.broadcasted_iota(jnp.int32, (segs, LANES), 0) + (zone * slab_count + slab) * segs
        own = own.astype(jnp.float32)
        total = jnp.zeros((segs, LANES), jnp.float32)
        for i in range(slab_count):
            hit = gathered_ref[i, segs : segs + 1, :] == own
            total = total + jnp.where(hit, gathered_ref[i, segs + 1 : segs + 2, :], 0.0)
        total = jnp.sum(total, axis=1, keepdims=True)
        out_ref[zone] = -total * gathered_ref[slab, :segs, :]

    @pl.when(zone == zone_count - 1)
    def _():
        for z in range(zone_count - 1):
            own = lax.broadcasted_iota(jnp.int32, (segs, fanout * segs), 0) + (z * slab_count + slab) * segs
            own = own.astype(jnp.float32)
            pickers, faces = [], []
            for i in range(slab_count):
                hit = gathered_ref[i, segs : segs + 1, :] == own
                pickers.append(jnp.where(hit, gathered_ref[i, segs + 1 : segs + 2, :], 0.0))
                faces.extend([gathered_ref[i, :segs, :]] * fanout)
            out_ref[z] = jnp.dot(
                jnp.concatenate(pickers, axis=1),
                jnp.concatenate(faces, axis=0),
                precision=HIGHEST,
                preferred_element_type=jnp.float32,
            )
        total = jnp.sum(weight, axis=1, keepdims=True)
        out_ref[zone_count - 1] = -total * gathered_ref[slab, :segs, :]


def stencil_kernel(
    diffusivity_ref, field_ref, speed_ref, out_ref, top_ref, bottom_ref, up_ref, down_ref,
    field, speed, result, field_sem, speed_sem, out_sem,
):
    _, tracer_count, rows, cols = field_ref.shape
    chunks = out_sem.shape[0]
    step = rows // chunks

    def cut(i):
        return pl.ds(i * step, step)

    loads = [pltpu.make_async_copy(field_ref.at[0, :, cut(i), :], field.at[:, cut(i), :], field_sem.at[i]) for i in range(chunks)]
    speeds = [pltpu.make_async_copy(speed_ref.at[0, :, cut(i), :], speed.at[:, cut(i), :], speed_sem.at[i]) for i in range(chunks)]
    stores = []
    for i in range(chunks):
        low, high = i * step, (i + 1) * step
        low, high = (TILE if i == 0 else low), (rows - TILE if i == chunks - 1 else high)
        piece = pl.ds(low, high - low)
        stores.append(pltpu.make_async_copy(result.at[:, piece, :], out_ref.at[0, :, piece, :], out_sem.at[i]))
    for i in range(chunks):
        loads[i].start()
        speeds[i].start()
    index = lax.broadcasted_iota(jnp.int32, (TILE, cols), 0)

    def tile(low, is_first, is_last, put):
        here = pl.ds(low, TILE)
        a, b = speed[0, here, :], speed[1, here, :]
        a_plus, b_plus = jnp.maximum(a, 0.0), jnp.maximum(b, 0.0)
        a_minus, b_minus = a_plus - a, b_plus - b
        rest = 1.0 - ((a_plus + a_minus) + (b_plus + b_minus))
        for t in range(tracer_count):
            d = diffusivity_ref[t]
            center = field[t, here, :]
            upper = pltpu.roll(center, 1, 0)
            lower = pltpu.roll(center, TILE - 1, 0)
            if is_first:
                upper = jnp.where(index == 0, 0.0, upper)
            else:
                upper = jnp.where(index == 0, pltpu.roll(field[t, pl.ds(low - TILE, TILE), :], 1, 0), upper)
            if is_last:
                lower = jnp.where(index == TILE - 1, 0.0, lower)
            else:
                lower = jnp.where(index == TILE - 1, pltpu.roll(field[t, pl.ds(low + TILE, TILE), :], TILE - 1, 0), lower)
            left = pltpu.roll(center, 1, 1)
            right = pltpu.roll(center, cols - 1, 1)
            up, down = a_plus + d, a_minus + d
            if is_first:
                up_ref[t : t + 1, :] = up[0:1, :]
            if is_last:
                down_ref[t : t + 1, :] = down[TILE - 1 : TILE, :]
            put(
                t,
                (rest - 4.0 * d) * center + up * upper + down * lower + (b_plus + d) * left + (b_minus + d) * right,
            )

    def put_top(t, value):
        top_ref[t] = value

    def put_bottom(t, value):
        bottom_ref[t] = value

    loads[0].wait()
    for i in range(chunks):
        if i + 1 < chunks:
            loads[i + 1].wait()
        speeds[i].wait()
        first, last = i * step // TILE, (i + 1) * step // TILE
        if i == 0:
            tile(0, True, False, put_top)
            first += 1
        if i == chunks - 1:
            last -= 1

        def body(r, carry):
            low = pl.multiple_of(r * TILE, TILE)

            def put(t, value):
                result[t, pl.ds(low, TILE), :] = value

            tile(low, False, False, put)
            return carry

        lax.fori_loop(first, last, body, 0)
        if i == chunks - 1:
            tile(rows - TILE, False, True, put_bottom)
        stores[i].start()
    for store in stores:
        store.wait()


def last_kernel(
    received_ref, gathered_ref, below_ref, top_ref, bottom_ref, up_ref, down_ref, partial_ref,
    out_ref, top, bottom, sem,
):
    zone_count, segs, _ = received_ref.shape
    tracer_count, _, cols = top_ref.shape
    rows = out_ref.shape[2]
    blocks = cols // LANES
    slab = lax.axis_index("slab")
    above = gathered_ref[jnp.maximum(slab - 1, 0), :segs, :]
    above = jnp.where(slab > 0, above, jnp.zeros_like(above))
    coupling = received_ref[0]
    for z in range(1, zone_count):
        coupling = coupling + received_ref[z]
    above = from_face(above, tracer_count)
    coupling = from_face(COUPLE * coupling, tracer_count)
    top[...] = top_ref[...]
    bottom[...] = bottom_ref[...]
    for t in range(tracer_count):
        for c in range(blocks):
            here = slice(c * LANES, (c + 1) * LANES)
            top[t, 0:1, here] = top[t, 0:1, here] + up_ref[t : t + 1, here] * above[t][c : c + 1, :]
            bottom[t, TILE - 1 : TILE, here] = (
                bottom[t, TILE - 1 : TILE, here]
                + down_ref[t : t + 1, here] * below_ref[t : t + 1, here]
                + coupling[t][c : c + 1, :]
            )
    first = pltpu.make_async_copy(top, out_ref.at[0, :, pl.ds(0, TILE), :], sem.at[0])
    second = pltpu.make_async_copy(bottom, out_ref.at[0, :, pl.ds(rows - TILE, TILE), :], sem.at[1])
    first.start()
    second.start()
    first.wait()
    second.wait()


def shards(tracers, velocity, diffusivity, owner_dev, owner_seg, intersection):
    zone_count = lax.axis_size("zone")
    slab_count = lax.axis_size("slab")
    _, tracer_count, rows, cols = tracers.shape
    segs = cols // SEG
    f32 = jnp.float32
    edge = (1, tracer_count, TILE, cols)
    tables = [pl.BlockSpec(table.shape, lambda i: (0, 0)) for table in (owner_dev, owner_seg, intersection)]
    payload, first = pl.pallas_call(
        pack_kernel,
        grid=(1,),
        out_shape=(
            jax.ShapeDtypeStruct((slab_count, segs + TILE, LANES), f32),
            jax.ShapeDtypeStruct((tracer_count, cols), f32),
        ),
        in_specs=[
            pl.BlockSpec(edge, lambda i: (0, 0, 0, 0)),
            pl.BlockSpec(edge, lambda i: (0, 0, rows // TILE - 1, 0)),
            *tables,
        ],
        out_specs=(
            pl.BlockSpec((slab_count, segs + TILE, LANES), lambda i: (0, 0, 0)),
            pl.BlockSpec((tracer_count, cols), lambda i: (0, 0)),
        ),
        scratch_shapes=[pltpu.VMEM((tracer_count, cols // LANES, LANES), f32)],
    )(tracers, tracers, owner_dev, owner_seg, intersection)
    below = lax.ppermute(first, "slab", [(i + 1, i) for i in range(slab_count - 1)])
    gathered = lax.all_to_all(payload, "slab", 0, 0, tiled=True)

    chunks = rows // 32
    edge_tile = jax.ShapeDtypeStruct((tracer_count, TILE, cols), f32)
    edge_row = jax.ShapeDtypeStruct((tracer_count, cols), f32)
    partial, top, bottom, up, down = pl.pallas_call(
        stencil_kernel,
        out_shape=(jax.ShapeDtypeStruct(tracers.shape, f32), edge_tile, edge_tile, edge_row, edge_row),
        in_specs=[SMEM, ANY, ANY],
        out_specs=(ANY, VMEM, VMEM, VMEM, VMEM),
        scratch_shapes=[
            pltpu.VMEM((tracer_count, rows, cols), f32),
            pltpu.VMEM((2, rows, cols), f32),
            pltpu.VMEM((tracer_count, rows, cols), f32),
            pltpu.SemaphoreType.DMA((chunks,)),
            pltpu.SemaphoreType.DMA((chunks,)),
            pltpu.SemaphoreType.DMA((chunks,)),
        ],
        compiler_params=pltpu.CompilerParams(vmem_limit_bytes=32 * 2**20),
        cost_estimate=pl.CostEstimate(
            flops=20 * tracers.size, transcendentals=0, bytes_accessed=4 * (2 * tracers.size + velocity.size)
        ),
    )(diffusivity, tracers, velocity)

    gathered, up = lax.optimization_barrier((gathered, up))
    partials = pl.pallas_call(
        middle_kernel,
        out_shape=jax.ShapeDtypeStruct((zone_count, segs, LANES), f32),
        in_specs=[VMEM] * 4,
        out_specs=VMEM,
    )(gathered, owner_dev, owner_seg, intersection)
    received = lax.all_to_all(partials, "zone", 0, 0, tiled=True)
    return pl.pallas_call(
        last_kernel,
        out_shape=jax.ShapeDtypeStruct(tracers.shape, f32),
        in_specs=[VMEM] * 7 + [ANY],
        out_specs=ANY,
        scratch_shapes=[
            pltpu.VMEM((tracer_count, TILE, cols), f32),
            pltpu.VMEM((tracer_count, TILE, cols), f32),
            pltpu.SemaphoreType.DMA((2,)),
        ],
        input_output_aliases={7: 0},
    )(received, gathered, below, top, bottom, up, down, partial)


def solution(mesh):
    placed = (
        P("zone", None, "slab", None),
        P("zone", None, "slab", None),
        P(),
        P("slab", None),
        P("slab", None),
        P("slab", None),
    )
    return jax.shard_map(
        shards, mesh=mesh, in_specs=placed, out_specs=P("zone", None, "slab", None), check_vma=False
    )
```

time: 118 us -> 45.5 us (0.39); the launches traced: 116 us -> 44.8 us
  blocking collectives: 46.5 us -> 0 us
  other arithmetic: 29.2 us -> 0 us
  Pallas kernels: 0 us -> 15.5 us
  between operations: 13.5 us -> 0.05 us
  starting transfers between devices: 2.85 us -> 11.9 us
  local copies, waits for them, and re-layouts: 22.2 us -> 13.6 us
  waiting for transfers between devices: 0.02 us -> 3.73 us
  matrix products: 1.48 us -> 0 us
    psum x2 -> x0, blocking collectives: 30.6 us -> none  [the longest x1 16.3 us: from_root(): return lax.psum(block, axis)]
    sub x2 -> x0, other arithmetic: 22 us -> none  [the longest x1 21.2 us: advance(): return center + diffusivity[None, :, None, None] * laplace - transport]
    all_gather x1 -> x0, blocking collectives: 15.9 us -> none  [shards(): zone_faces = lax.all_gather(own_face, 'slab', axis=0, tiled=True)]
    slice x3 -> x0, local copies, waits for them, and re-layouts: 15.9 us -> none  [the longest x2 14.7 us: advance(): left_cells = jnp.roll(center, 1, axis=3)]
    pallas_call x0 -> x4, Pallas kernels: none -> 15.5 us  [the longest x1 9.42 us: shards(): pl.pallas_call(stencil_kernel, out_shape=(jax.ShapeDtypeStruct(tracers.sh...]
    unnamed x9 -> x25, local copies, waits for them, and re-layouts: 2.32 us -> 13.6 us
    all_to_all x0 -> x2, starting transfers between devices: none -> 10.6 us  [the longest x1 6.46 us: shards(): gathered = lax.all_to_all(payload, 'slab', 0, 0, tiled=True)]
    another operation x3 -> x0, other arithmetic: 4.17 us -> none
  transfers between devices with their start and end apart: 3 -> 3, of which waited for: 0 -> 2; matrix products, arithmetic and copies ran while one was open for 36% -> 0% of each run, Pallas kernels for 0% -> 21%
where the time goes in v1:
time: 45.5 us; the launch traced here: 44.8 us
  Pallas kernels  15.5 us (34%)
  local copies, waits for them, and re-layouts  13.6 us (30%)
  starting transfers between devices  11.9 us (26%)
  waiting for transfers between devices  3.73 us (8%)
    unnamed x25, local copies, waits for them, and re-layouts  13.6 us
    pallas_call x1, Pallas kernels, shards(): pl.pallas_call(stencil_kernel, out_shape=(jax.ShapeDtypeStruct(tracers.sh...  9.42 us
    all_to_all x1, starting transfers between devices, shards(): gathered = lax.all_to_all(payload, 'slab', 0, 0, tiled=True)  6.46 us
    all_to_all x1, starting transfers between devices, shards(): received = lax.all_to_all(partials, 'zone', 0, 0, tiled=True)  4.19 us
    pallas_call x1, Pallas kernels, shards(): pl.pallas_call(last_kernel, out_shape=jax.ShapeDtypeStruct(tracers.shape,...  2.14 us
    pallas_call x1, Pallas kernels, shards(): pl.pallas_call(middle_kernel, out_shape=jax.ShapeDtypeStruct((zone_count,...  1.97 us
    pallas_call x1, Pallas kernels, shards(): pl.pallas_call(pack_kernel, grid=(1,), out_shape=(jax.ShapeDtypeStruct((s...  1.94 us
    all_to_all x1, waiting for transfers between devices, shards(): received = lax.all_to_all(partials, 'zone', 0, 0, tiled=True)  1.93 us
  transfers between devices with their start and end apart: 3, of which 2 were waited for; matrix products, arithmetic and copies ran while one was open for 0% of the time, Pallas kernels for 21%

profile of v1, /device:TPU:0, one launch (start us, length us, event | category | flops | bytes accessed | tf_op | source)
XLA Modules:
  0.0 44.8 jit_solution(11139720969567429381)
XLA Ops:
  0.0 1.4 %copy.8.dev_ref = s32[64,2]{1,0:T(8,128)} copy(s32[64,2]{0,1:T(2,128)} %param.9) | data formatting | bytes 1024 | tf_op args[3]
  1.4 1.4 %copy.9.seg_ref = s32[64,2]{1,0:T(8,128)} copy(s32[64,2]{0,1:T(2,128)} %param.10) | data formatting | bytes 1024 | tf_op args[4]
  2.7 1.4 %copy.10.weight_ref = f32[64,2]{1,0:T(8,128)} copy(f32[64,2]{0,1:T(2,128)} %param.11) | data formatting | bytes 1024 | tf_op args[5]
  4.1 0.0 copy-start.6
  4.1 1.9 %shard_map.64 = (f32[8,72,128]{2,1,0:T(8,128)}, f32[4,2048]{1,0:T(4,128)}) custom-call(f32[1,4,256,2048]{3,2,1,0:T(8,128)} %field_ref.1, f32[1,4,256,2048]{3,2,1,0:T(8,128)} %field_ref.1, s32[64,2]{1,0:T(8,128)} %copy.8.dev_ref, s32[64,2]{1,0:T(8,128)} %copy.9.seg_ref, f32[64,2]{1,0:T(8,128)} %copy.10.weight_ref), custom_call_target="tpu_custom_call" | custom-call | tf_op jit(solution)/shard_map/pallas_call | solution.py:272
  6.0 0.0 copy-start.10
  6.0 6.5 %all-to-all-start = ((f32[8,72,128]{2,1,0:T(8,128)}), f32[8,72,128]{2,1,0:T(8,128)S(1)}, u32[]{:S(2)}, u32[]{:S(2)}) async-start(f32[8,72,128]{2,1,0:T(8,128)} %get-tuple-element.14), calls=%async_computation | async-start | bytes 589824 | tf_op jit(solution)/shard_map/all_to_all | solution.py:291
  12.5 0.0 copy-done.6
  12.5 0.0 copy-start
  12.5 3.4 %copy-done = f32[1,4,256,2048]{3,2,1,0:T(8,128)S(1)} copy-done((f32[1,4,256,2048]{3,2,1,0:T(8,128)S(1)}, f32[1,4,256,2048]{3,2,1,0:T(8,128)}, u32[]{:S(2)}) %copy-start) | copy-done | bytes 8388632
  15.9 0.0 copy-start.1
  15.9 2.2 %copy-done.1 = f32[1,2,256,2048]{3,2,1,0:T(8,128)S(1)} copy-done((f32[1,2,256,2048]{3,2,1,0:T(8,128)S(1)}, f32[1,2,256,2048]{3,2,1,0:T(8,128)}, u32[]{:S(2)}) %copy-start.1) | copy-done | bytes 4194328
  18.1 9.4 %shard_map.65 = (f32[1,4,256,2048]{3,2,1,0:T(8,128)}, f32[4,8,2048]{2,1,0:T(8,128)S(1)}, f32[4,8,2048]{2,1,0:T(8,128)S(1)}, f32[4,2048]{1,0:T(4,128)S(1)}, f32[4,2048]{1,0:T(4,128)S(1)}) custom-call(f32[4]{0:T(128)S(1)} %copy-done.6, f32[1,4,256,2048]{3,2,1,0:T(8,128)S(1)} %copy-done, f32[1,2,256,2048]{3,2,1,0:T(8,128)S(1)} %copy-done.1), custom_call_target="tpu_custom_call" | custom-call | flops 41943040 | bytes 20971520 | tf_op jit(solution)/shard_map/pallas_call | solution.py:296
  27.5 0.0 copy-start.2
  27.5 0.7 %copy-done.2 = f32[4,8,2048]{2,1,0:T(8,128)} copy-done((f32[4,8,2048]{2,1,0:T(8,128)}, f32[4,8,2048]{2,1,0:T(8,128)S(1)}, u32[]{:S(2)}) %copy-start.2) | copy-done | bytes 262168
  28.2 0.0 copy-start.3
  28.2 0.7 %copy-done.3 = f32[4,8,2048]{2,1,0:T(8,128)} copy-done((f32[4,8,2048]{2,1,0:T(8,128)}, f32[4,8,2048]{2,1,0:T(8,128)S(1)}, u32[]{:S(2)}) %copy-start.3) | copy-done | bytes 262168
  28.9 0.0 copy-start.4
  28.9 0.6 %copy-done.4 = f32[4,2048]{1,0:T(4,128)} copy-done((f32[4,2048]{1,0:T(4,128)}, f32[4,2048]{1,0:T(4,128)S(1)}, u32[]{:S(2)}) %copy-start.4) | copy-done | bytes 32792
  29.5 0.0 copy-start.5
  29.5 0.6 %copy-done.5 = f32[4,2048]{1,0:T(4,128)} copy-done((f32[4,2048]{1,0:T(4,128)}, f32[4,2048]{1,0:T(4,128)S(1)}, u32[]{:S(2)}) %copy-start.5) | copy-done | bytes 32792
  30.1 0.0 all-to-all-done.gathered_ref
  30.1 0.0 copy-start.7
  30.1 0.7 %copy-done.7 = f32[8,72,128]{2,1,0:T(8,128)} copy-done((f32[8,72,128]{2,1,0:T(8,128)}, f32[8,72,128]{2,1,0:T(8,128)S(1)}, u32[]{:S(2)}) %copy-start.7) | copy-done | bytes 294936
  30.8 2.0 %shard_map.66 = f32[4,64,128]{2,1,0:T(8,128)} custom-call(f32[8,72,128]{2,1,0:T(8,128)} %copy-done.7, s32[64,2]{1,0:T(8,128)} %copy.8.dev_ref, s32[64,2]{1,0:T(8,128)} %copy.9.seg_ref, f32[64,2]{1,0:T(8,128)} %copy.10.weight_ref), custom_call_target="tpu_custom_call" | custom-call | tf_op jit(solution)/shard_map/pallas_call | solution.py:316
  32.8 4.2 %all-to-all-start.1 = ((f32[4,64,128]{2,1,0:T(8,128)}), f32[4,64,128]{2,1,0:T(8,128)S(1)}, u32[]{:S(2)}, u32[]{:S(2)}) async-start(f32[4,64,128]{2,1,0:T(8,128)} %shard_map.66), calls=%async_computation.1 | async-start | bytes 262144 | tf_op jit(solution)/shard_map/all_to_all | solution.py:322
  37.0 0.0 copy-done.10
  37.0 1.3 %collective-permute-start = (f32[4,2048]{1,0:T(4,128)S(1)}, f32[4,2048]{1,0:T(4,128)S(1)}, u32[]{:S(2)}, u32[]{:S(2)}) collective-permute-start(f32[4,2048]{1,0:T(4,128)S(1)} %copy-done.10), channel_id=1, source_target_pairs={{1,0},{2,1},{3,2},{4,3},{5,4},{6,5},{7,6},{9,8},{10,9},{11,10},{12... | collective-permute-start | bytes 98312 | tf_op jit(solution)/shard_map/ppermute | solution.py:290
  38.3 1.8 %collective-permute-done.below_ref = f32[4,2048]{1,0:T(4,128)S(1)} collective-permute-done((f32[4,2048]{1,0:T(4,128)S(1)}, f32[4,2048]{1,0:T(4,128)S(1)}, u32[]{:S(2)}, u32[]{:S(2)}) %collective-permute-start) | collective-permute-done | bytes 32800 | tf_op jit(solution)/shard_map/ppermute | solution.py:290
  40.1 0.0 copy-start.9
  40.1 1.9 %all-to-all-done.1.received_ref = f32[4,64,128]{2,1,0:T(8,128)S(1)} async-done(((f32[4,64,128]{2,1,0:T(8,128)}), f32[4,64,128]{2,1,0:T(8,128)S(1)}, u32[]{:S(2)}, u32[]{:S(2)}) %all-to-all-start.1) | async-done | bytes 131104 | tf_op jit(solution)/shard_map/all_to_all | solution.py:322
  42.0 0.0 copy-start.8
  42.0 0.0 copy-done.9
  42.0 0.6 %copy-done.8 = f32[4,64,128]{2,1,0:T(8,128)} copy-done((f32[4,64,128]{2,1,0:T(8,128)}, f32[4,64,128]{2,1,0:T(8,128)S(1)}, u32[]{:S(2)}) %copy-start.8) | copy-done | bytes 131096
  42.6 2.1 %shard_map.67 = f32[1,4,256,2048]{3,2,1,0:T(8,128)} custom-call(f32[4,64,128]{2,1,0:T(8,128)} %copy-done.8, f32[8,72,128]{2,1,0:T(8,128)} %copy-done.7, f32[4,2048]{1,0:T(4,128)} %copy-done.9, f32[4,8,2048]{2,1,0:T(8,128)} %copy-done.2, f32[4,8,2048]{2,1,0:T(8,128)} %copy-done.3, f32[4,2048]{1,0:T(4,128)} %copy-done.4, ...), custom_call_target="tpu_custom_call", output_to_operand_aliasing={{}: (7, {})} | custom-call | tf_op jit(solution)/shard_map/pallas_call | solution.py:323
Async XLA Ops:
  4.1 8.4 %copy-start.6 = (f32[4]{0:T(128)S(1)}, f32[4]{0:T(128)}, u32[]{:S(2)}) copy-start(f32[4]{0:T(128)} %diffusivity_ref.1) | copy-start | bytes 52
  6.0 30.9 %copy-start.10 = (f32[4,2048]{1,0:T(4,128)S(1)}, f32[4,2048]{1,0:T(4,128)}, u32[]{:S(2)}) copy-start(f32[4,2048]{1,0:T(4,128)} %get-tuple-element.17) | copy-start | bytes 98308
  6.0 24.1 %all-to-all-start = ((f32[8,72,128]{2,1,0:T(8,128)}), f32[8,72,128]{2,1,0:T(8,128)S(1)}, u32[]{:S(2)}, u32[]{:S(2)}) async-start(f32[8,72,128]{2,1,0:T(8,128)} %get-tuple-element.14), calls=%async_computation | async-start | bytes 589824 | tf_op jit(solution)/shard_map/all_to_all | solution.py:291
  12.5 3.4 %copy-start = (f32[1,4,256,2048]{3,2,1,0:T(8,128)S(1)}, f32[1,4,256,2048]{3,2,1,0:T(8,128)}, u32[]{:S(2)}) copy-start(f32[1,4,256,2048]{3,2,1,0:T(8,128)} %field_ref.1) | copy-start | bytes 25165828
  15.9 2.2 %copy-start.1 = (f32[1,2,256,2048]{3,2,1,0:T(8,128)S(1)}, f32[1,2,256,2048]{3,2,1,0:T(8,128)}, u32[]{:S(2)}) copy-start(f32[1,2,256,2048]{3,2,1,0:T(8,128)} %speed_ref.1) | copy-start | bytes 12582916
  27.5 0.7 %copy-start.2 = (f32[4,8,2048]{2,1,0:T(8,128)}, f32[4,8,2048]{2,1,0:T(8,128)S(1)}, u32[]{:S(2)}) copy-start(f32[4,8,2048]{2,1,0:T(8,128)S(1)} %get-tuple-element.18.top_ref) | copy-start | bytes 786436
  28.2 0.7 %copy-start.3 = (f32[4,8,2048]{2,1,0:T(8,128)}, f32[4,8,2048]{2,1,0:T(8,128)S(1)}, u32[]{:S(2)}) copy-start(f32[4,8,2048]{2,1,0:T(8,128)S(1)} %get-tuple-element.19.bottom_ref) | copy-start | bytes 786436
  28.9 0.6 %copy-start.4 = (f32[4,2048]{1,0:T(4,128)}, f32[4,2048]{1,0:T(4,128)S(1)}, u32[]{:S(2)}) copy-start(f32[4,2048]{1,0:T(4,128)S(1)} %get-tuple-element.20.up_ref) | copy-start | bytes 98308
  29.5 0.6 %copy-start.5 = (f32[4,2048]{1,0:T(4,128)}, f32[4,2048]{1,0:T(4,128)S(1)}, u32[]{:S(2)}) copy-start(f32[4,2048]{1,0:T(4,128)S(1)} %get-tuple-element.21.down_ref) | copy-start | bytes 98308
  30.1 0.7 %copy-start.7 = (f32[8,72,128]{2,1,0:T(8,128)}, f32[8,72,128]{2,1,0:T(8,128)S(1)}, u32[]{:S(2)}) copy-start(f32[8,72,128]{2,1,0:T(8,128)S(1)} %all-to-all-done.gathered_ref) | copy-start | bytes 884740
  32.8 9.2 %all-to-all-start.1 = ((f32[4,64,128]{2,1,0:T(8,128)}), f32[4,64,128]{2,1,0:T(8,128)S(1)}, u32[]{:S(2)}, u32[]{:S(2)}) async-start(f32[4,64,128]{2,1,0:T(8,128)} %shard_map.66), calls=%async_computation.1 | async-start | bytes 262144 | tf_op jit(solution)/shard_map/all_to_all | solution.py:322
  37.0 3.1 %collective-permute-start = (f32[4,2048]{1,0:T(4,128)S(1)}, f32[4,2048]{1,0:T(4,128)S(1)}, u32[]{:S(2)}, u32[]{:S(2)}) collective-permute-start(f32[4,2048]{1,0:T(4,128)S(1)} %copy-done.10), channel_id=1, source_target_pairs={{1,0},{2,1},{3,2},{4,3},{5,4},{6,5},{7,6},{9,8},{10,9},{11,10},{12... | collective-permute-start | bytes 98312 | tf_op jit(solution)/shard_map/ppermute | solution.py:290
  40.1 1.9 %copy-start.9 = (f32[4,2048]{1,0:T(4,128)}, f32[4,2048]{1,0:T(4,128)S(1)}, u32[]{:S(2)}) copy-start(f32[4,2048]{1,0:T(4,128)S(1)} %collective-permute-done.below_ref) | copy-start | bytes 98308
  42.0 0.6 %copy-start.8 = (f32[4,64,128]{2,1,0:T(8,128)}, f32[4,64,128]{2,1,0:T(8,128)S(1)}, u32[]{:S(2)}) copy-start(f32[4,64,128]{2,1,0:T(8,128)S(1)} %all-to-all-done.1.received_ref) | copy-start | bytes 393220

commit v2 on v1

--- a/solution.py
+++ b/solution.py
@@ -52,30 +52,36 @@
     return rows
 
 
-def pack_kernel(top_ref, bottom_ref, dev_ref, seg_ref, weight_ref, out_ref, first_ref, rows_ref):
+def pack_kernel(top_ref, bottom_ref, dev_ref, seg_ref, weight_ref, out_ref, first_ref, own_ref, rows_ref):
     tracer_count, _, cols = bottom_ref.shape[1:]
     blocks = cols // LANES
-    segs = dev_ref.shape[0]
+    fanout, segs = dev_ref.shape
     for t in range(tracer_count):
         first_ref[t : t + 1, :] = top_ref[0, t, 0:1, :]
         for c in range(blocks):
             rows_ref[t, c : c + 1, :] = bottom_ref[0, t, TILE - 1 : TILE, c * LANES : (c + 1) * LANES]
     face = to_face([rows_ref[t] for t in range(tracer_count)])
-    lane = lax.broadcasted_iota(jnp.int32, (segs, LANES), 1)
-    row = lax.broadcasted_iota(jnp.int32, (segs, LANES), 0)
-    mine = lane % segs == permuted(row, blocks)
-    target = dev_ref[...] * segs + permuted(seg_ref[...], blocks)
-    target = target.astype(jnp.float32)
-    weight = weight_ref[...]
-    fanout = target.shape[1]
-
-    def in_lanes(table):
-        picked = table[:, 0:1]
-        for k in range(1, fanout):
-            picked = jnp.where(lane < k * segs, picked, table[:, k : k + 1])
-        return jnp.sum(jnp.where(mine, picked, 0.0), axis=0, keepdims=True)
-
-    targets, weights = in_lanes(target), in_lanes(weight)
+    lane = lax.broadcasted_iota(jnp.int32, (segs, segs), 1)
+    row = lax.broadcasted_iota(jnp.int32, (segs, segs), 0)
+    source = lane == (row % blocks) * (LANES // SEG) + row // blocks
+    target = (dev_ref[...] * segs + permuted(seg_ref[...], blocks)).astype(jnp.float32)
+    index = lax.broadcasted_iota(jnp.int32, (segs, LANES), 1)
+    order = lax.broadcasted_iota(jnp.int32, (segs, LANES), 0)
+
+    def columns(table):
+        return [jnp.sum(jnp.where(source, table[k : k + 1, :], 0.0), axis=1, keepdims=True) for k in range(fanout)]
+
+    targets, weights = columns(target), columns(weight_ref[...])
+    own_ref[...] = jnp.zeros_like(own_ref)
+    lines = []
+    for k, column in enumerate([*targets, *weights]):
+        own_ref[:, k : k + 1] = column
+    for table in (targets, weights):
+        line = 0.0
+        for k, column in enumerate(table):
+            line = line + jnp.where(index == k * segs + order, column, 0.0)
+        lines.append(jnp.sum(line, axis=0, keepdims=True))
+    targets, weights = lines
     index = lax.broadcasted_iota(jnp.int32, (TILE, LANES), 0)
     tables = jnp.where(index == 0, targets, jnp.where(index == 1, weights, 0.0))
     for slab in range(out_ref.shape[0]):
@@ -84,27 +90,21 @@
         out_ref[slab, segs : segs + TILE, :] = tables
 
 
-def middle_kernel(gathered_ref, dev_ref, seg_ref, weight_ref, out_ref):
+def middle_kernel(gathered_ref, own_ref, out_ref):
     slab_count = gathered_ref.shape[0]
     zone_count, segs, _ = out_ref.shape
-    fanout = dev_ref.shape[1]
-    quarters = LANES // SEG
-    blocks = segs // quarters
+    fanout = LANES // segs
     zone, slab = lax.axis_index("zone"), lax.axis_index("slab")
     out_ref[...] = jnp.zeros_like(out_ref)
 
-    def reordered(ref):
-        return jnp.concatenate([ref[pl.ds(u, blocks, stride=quarters), :] for u in range(quarters)], axis=0)
-
-    weight = reordered(weight_ref)
-
     @pl.when(zone < zone_count - 1)
     def _():
-        target = reordered(dev_ref) * segs + permuted(reordered(seg_ref), blocks)
         slots = lax.broadcasted_iota(jnp.int32, (segs, slab_count * segs), 1) + zone * (slab_count * segs)
+        slots = slots.astype(jnp.float32)
         picker = jnp.zeros(slots.shape, jnp.float32)
         for k in range(fanout):
-            picker = picker + jnp.where(target[:, k : k + 1] == slots, weight[:, k : k + 1], 0.0)
+            target, weight = own_ref[:, k : k + 1], own_ref[:, fanout + k : fanout + k + 1]
+            picker = picker + jnp.where(target == slots, weight, 0.0)
         faces = jnp.concatenate([gathered_ref[i, :segs, :] for i in range(slab_count)], axis=0)
         out_ref[zone_count - 1] = jnp.dot(picker, faces, precision=HIGHEST, preferred_element_type=jnp.float32)
         own = lax.broadcasted_iota(jnp.int32, (segs, LANES), 0) + (zone * slab_count + slab) * segs
@@ -132,7 +132,7 @@
                 precision=HIGHEST,
                 preferred_element_type=jnp.float32,
             )
-        total = jnp.sum(weight, axis=1, keepdims=True)
+        total = jnp.sum(own_ref[:, fanout : 2 * fanout], axis=1, keepdims=True)
         out_ref[zone_count - 1] = -total * gathered_ref[slab, :segs, :]
 
 
@@ -267,14 +267,20 @@
     _, tracer_count, rows, cols = tracers.shape
     segs = cols // SEG
     f32 = jnp.float32
+    small = pltpu.CompilerParams(vmem_limit_bytes=8 * 2**20)
     edge = (1, tracer_count, TILE, cols)
+    tracers, velocity, owner_dev, owner_seg, intersection = (
+        pltpu.with_memory_space_constraint(x, pltpu.HBM)
+        for x in (tracers, velocity, owner_dev.T, owner_seg.T, intersection.T)
+    )
     tables = [pl.BlockSpec(table.shape, lambda i: (0, 0)) for table in (owner_dev, owner_seg, intersection)]
-    payload, first = pl.pallas_call(
+    payload, first, own = pl.pallas_call(
         pack_kernel,
         grid=(1,),
         out_shape=(
             jax.ShapeDtypeStruct((slab_count, segs + TILE, LANES), f32),
             jax.ShapeDtypeStruct((tracer_count, cols), f32),
+            jax.ShapeDtypeStruct((segs, LANES), f32),
         ),
         in_specs=[
             pl.BlockSpec(edge, lambda i: (0, 0, 0, 0)),
@@ -284,7 +290,9 @@
         out_specs=(
             pl.BlockSpec((slab_count, segs + TILE, LANES), lambda i: (0, 0, 0)),
             pl.BlockSpec((tracer_count, cols), lambda i: (0, 0)),
+            pl.BlockSpec((segs, LANES), lambda i: (0, 0)),
         ),
+        compiler_params=small,
         scratch_shapes=[pltpu.VMEM((tracer_count, cols // LANES, LANES), f32)],
     )(tracers, tracers, owner_dev, owner_seg, intersection)
     below = lax.ppermute(first, "slab", [(i + 1, i) for i in range(slab_count - 1)])
@@ -312,13 +320,14 @@
         ),
     )(diffusivity, tracers, velocity)
 
-    gathered, up = lax.optimization_barrier((gathered, up))
+    gathered, below, up = lax.optimization_barrier((gathered, below, up))
     partials = pl.pallas_call(
         middle_kernel,
         out_shape=jax.ShapeDtypeStruct((zone_count, segs, LANES), f32),
-        in_specs=[VMEM] * 4,
+        in_specs=[VMEM] * 2,
         out_specs=VMEM,
-    )(gathered, owner_dev, owner_seg, intersection)
+        compiler_params=small,
+    )(gathered, own)
     received = lax.all_to_all(partials, "zone", 0, 0, tiled=True)
     return pl.pallas_call(
         last_kernel,
@@ -330,6 +339,7 @@
             pltpu.VMEM((tracer_count, TILE, cols), f32),
             pltpu.SemaphoreType.DMA((2,)),
         ],
+        compiler_params=small,
         input_output_aliases={7: 0},
     )(received, gathered, below, top, bottom, up, down, partial)
 

time: 45.5 us -> 30.8 us (0.68)
  local copies, waits for them, and re-layouts: 13.6 us -> 0.01 us
  blocking collectives: 0 us -> 9.36 us
  starting transfers between devices: 11.9 us -> 7.61 us
  waiting for transfers between devices: 3.73 us -> 0.01 us
  Pallas kernels: 15.5 us -> 13.5 us
    unnamed x25 -> x2, local copies, waits for them, and re-layouts: 13.6 us -> 0.01 us
    all_to_all x0 -> x1, blocking collectives: none -> 9.36 us  [shards(): received = lax.all_to_all(partials, 'zone', 0, 0, tiled=True)]
    all_to_all x1 -> x0, starting transfers between devices: 4.19 us -> none  [shards(): received = lax.all_to_all(partials, 'zone', 0, 0, tiled=True)]
    all_to_all x1 -> x0, waiting for transfers between devices: 1.93 us -> none  [shards(): received = lax.all_to_all(partials, 'zone', 0, 0, tiled=True)]
    ppermute x1, waiting for transfers between devices: 1.8 us -> 0.01 us  [shards(): lax.ppermute(first, 'slab', [(i + 1, i) for i in range(slab_count - 1)])]
    pallas_call x1, Pallas kernels: 1.97 us -> 0.35 us  [shards(): pl.pallas_call(middle_kernel, out_shape=jax.ShapeDtypeStruct((zone_count,...]
    pallas_call x1, Pallas kernels: 2.14 us -> 0.95 us  [shards(): pl.pallas_call(last_kernel, out_shape=jax.ShapeDtypeStruct(tracers.shape,...]
    pallas_call x1, Pallas kernels: 9.42 us -> 10.3 us  [shards(): pl.pallas_call(stencil_kernel, out_shape=(jax.ShapeDtypeStruct(tracers.sh...]
  transfers between devices with their start and end apart: 3 -> 2, of which waited for: 2 -> 0; matrix products, arithmetic and copies ran while one was open for 0% -> 0% of each run, Pallas kernels for 21% -> 34%
where the time goes in v2:
time: 30.8 us; the launch traced here: 30.5 us
  Pallas kernels  13.5 us (44%)
  blocking collectives  9.36 us (30%)
  starting transfers between devices  7.61 us (25%)
    pallas_call x1, Pallas kernels, shards(): pl.pallas_call(stencil_kernel, out_shape=(jax.ShapeDtypeStruct(tracers.sh...  10.3 us
    all_to_all x1, blocking collectives, shards(): received = lax.all_to_all(partials, 'zone', 0, 0, tiled=True)  9.36 us
    all_to_all x1, starting transfers between devices, shards(): gathered = lax.all_to_all(payload, 'slab', 0, 0, tiled=True)  6.33 us
    pallas_call x1, Pallas kernels, shards(): pl.pallas_call(pack_kernel, grid=(1,), out_shape=(jax.ShapeDtypeStruct((s...  1.95 us
    ppermute x1, starting transfers between devices, shards(): lax.ppermute(first, 'slab', [(i + 1, i) for i in range(slab_count - 1)])  1.28 us
    pallas_call x1, Pallas kernels, shards(): pl.pallas_call(last_kernel, out_shape=jax.ShapeDtypeStruct(tracers.shape,...  0.95 us
  transfers between devices with their start and end apart: 2, of which 0 were waited for; matrix products, arithmetic and copies ran while one was open for 0% of the time, Pallas kernels for 34%

profile of v2, /device:TPU:0, one launch (start us, length us, event | category | flops | bytes accessed | tf_op | source)
XLA Modules:
  0.0 30.5 jit_solution(15858358009119517393)
XLA Ops:
  0.0 0.0 copy-start
  0.0 2.0 %shard_map.64 = (f32[8,72,128]{2,1,0:T(8,128)}, f32[4,2048]{1,0:T(4,128)S(1)}, f32[64,128]{1,0:T(8,128)S(1)}) custom-call(f32[1,4,256,2048]{3,2,1,0:T(8,128)} %field_ref.1, f32[1,4,256,2048]{3,2,1,0:T(8,128)} %field_ref.1, s32[2,64]{1,0:T(2,128)} %bitcast.3, s32[2,64]{1,0:T(2,128)} %bitcast.4, f32[2,64]{1,0:T(2,128)} %bitcast.5), custom_call_target="tpu_custom_call" | custom-call | tf_op jit(solution)/shard_map/pallas_call | solution.py:277
  2.0 6.3 %all-to-all-start = ((f32[8,72,128]{2,1,0:T(8,128)}), f32[8,72,128]{2,1,0:T(8,128)S(1)}, u32[]{:S(2)}, u32[]{:S(2)}) async-start(f32[8,72,128]{2,1,0:T(8,128)} %get-tuple-element.16), calls=%async_computation | async-start | bytes 589824 | tf_op jit(solution)/shard_map/all_to_all | solution.py:299
  8.3 1.3 %collective-permute-start = (f32[4,2048]{1,0:T(4,128)S(1)}, f32[4,2048]{1,0:T(4,128)S(1)}, u32[]{:S(2)}, u32[]{:S(2)}) collective-permute-start(f32[4,2048]{1,0:T(4,128)S(1)} %get-tuple-element.17), channel_id=1, source_target_pairs={{1,0},{2,1},{3,2},{4,3},{5,4},{6,5},{7,6},{9,8},{10,9},{11,10},{12... | collective-permute-start | bytes 98312 | tf_op jit(solution)/shard_map/ppermute | solution.py:298
  9.6 0.0 copy-done
  9.6 10.3 %shard_map.65 = (f32[1,4,256,2048]{3,2,1,0:T(8,128)}, f32[4,8,2048]{2,1,0:T(8,128)S(1)}, f32[4,8,2048]{2,1,0:T(8,128)S(1)}, f32[4,2048]{1,0:T(4,128)S(1)}, f32[4,2048]{1,0:T(4,128)S(1)}) custom-call(f32[4]{0:T(128)S(1)} %copy-done, f32[1,4,256,2048]{3,2,1,0:T(8,128)} %field_ref.1, f32[1,2,256,2048]{3,2,1,0:T(8,128)} %speed_ref.1), custom_call_target="tpu_custom_call" | custom-call | flops 41943040 | bytes 20971520 | tf_op jit(solution)/shard_map/pallas_call | solution.py:304
  19.9 0.0 collective-permute-done.below_ref
  19.9 0.0 all-to-all-done.gathered_ref
  19.9 0.4 %shard_map.66 = f32[4,64,128]{2,1,0:T(8,128)S(1)} custom-call(f32[8,72,128]{2,1,0:T(8,128)S(1)} %all-to-all-done.gathered_ref, f32[64,128]{1,0:T(8,128)S(1)} %get-tuple-element.20.own_ref), custom_call_target="tpu_custom_call" | custom-call | tf_op jit(solution)/shard_map/pallas_call | solution.py:324
  20.2 9.4 %all_to_all.10.received_ref = f32[4,64,128]{2,1,0:T(8,128)S(1)} all-to-all(f32[4,64,128]{2,1,0:T(8,128)S(1)} %shard_map.66), channel_id=1, replica_groups=mesh['zone'=4,'slab'=8] {'zone'}, dimensions={0} | all-to-all | bytes 262144 | tf_op jit(solution)/shard_map/all_to_all | solution.py:331
  29.6 0.9 %shard_map.67 = f32[1,4,256,2048]{3,2,1,0:T(8,128)} custom-call(f32[4,64,128]{2,1,0:T(8,128)S(1)} %all_to_all.10.received_ref, f32[8,72,128]{2,1,0:T(8,128)S(1)} %all-to-all-done.gathered_ref, f32[4,2048]{1,0:T(4,128)S(1)} %collective-permute-done.below_ref, f32[4,8,2048]{2,1,0:T(8,128)S(1)} %get-tuple-element.22.top_ref, ...), custom_call_target="tpu_custom_call", output_to_operand_aliasing={{}: (7, {})} | custom-call | tf_op jit(solution)/shard_map/pallas_call | solution.py:332
Async XLA Ops:
  0.0 9.6 %copy-start = (f32[4]{0:T(128)S(1)}, f32[4]{0:T(128)}, u32[]{:S(2)}) copy-start(f32[4]{0:T(128)} %diffusivity_ref.1) | copy-start | bytes 52
  2.0 17.9 %all-to-all-start = ((f32[8,72,128]{2,1,0:T(8,128)}), f32[8,72,128]{2,1,0:T(8,128)S(1)}, u32[]{:S(2)}, u32[]{:S(2)}) async-start(f32[8,72,128]{2,1,0:T(8,128)} %get-tuple-element.16), calls=%async_computation | async-start | bytes 589824 | tf_op jit(solution)/shard_map/all_to_all | solution.py:299
  8.3 11.6 %collective-permute-start = (f32[4,2048]{1,0:T(4,128)S(1)}, f32[4,2048]{1,0:T(4,128)S(1)}, u32[]{:S(2)}, u32[]{:S(2)}) collective-permute-start(f32[4,2048]{1,0:T(4,128)S(1)} %get-tuple-element.17), channel_id=1, source_target_pairs={{1,0},{2,1},{3,2},{4,3},{5,4},{6,5},{7,6},{9,8},{10,9},{11,10},{12... | collective-permute-start | bytes 98312 | tf_op jit(solution)/shard_map/ppermute | solution.py:298

commit v3 on v0

v3 whole, which is shorter than its diff:
```python
import functools

import jax
import jax.numpy as jnp
from jax import lax
from jax.experimental import pallas as pl
from jax.experimental.pallas import tpu as pltpu
from jax.sharding import PartitionSpec as P

SEG = 32
LANES = 128
TILE = 8
COUPLE = 0.5
GROUP = 32
PIN = 3
UNROLL = 16
PIECES = (2, 5, 5, 7)
HIGHEST = lax.Precision.HIGHEST
VMEM = pl.BlockSpec(memory_space=pltpu.VMEM)
SMEM = pl.BlockSpec(memory_space=pltpu.SMEM)
ANY = pl.BlockSpec(memory_space=pl.ANY)


def permuted(segment, blocks):
    quarters = LANES // SEG
    return (segment % quarters) * blocks + segment // quarters


def lane_group(shape):
    return lax.broadcasted_iota(jnp.int32, shape, len(shape) - 1) // SEG


def to_face(rows):
    quarters = LANES // SEG
    out = []
    for u in range(quarters):
        face = None
        for t, row in enumerate(rows):
            moved = row if t == u else pltpu.roll(row, ((t - u) * SEG) % LANES, 1)
            face = moved if face is None else jnp.where(lane_group(row.shape) == t, moved, face)
        out.append(face)
    return out


def from_face(face, tracer_count):
    quarters = LANES // SEG
    blocks = face.shape[0] // quarters
    rows = []
    for t in range(tracer_count):
        row = None
        for u in range(quarters):
            part = face[u * blocks : (u + 1) * blocks]
            moved = part if t == u else pltpu.roll(part, ((u - t) * SEG) % LANES, 1)
            row = moved if row is None else jnp.where(lane_group(part.shape) == u, moved, row)
        rows.append(row)
    return rows


def pack_kernel(top_ref, bottom_ref, dev_ref, seg_ref, weight_ref, out_ref, own_ref, rows_ref):
    tracer_count, _, cols = bottom_ref.shape[1:]
    blocks = cols // LANES
    fanout, segs = dev_ref.shape
    for start, row, ref in ((0, TILE - 1, bottom_ref), (segs + TILE, 0, top_ref)):
        for t in range(tracer_count):
            for c in range(blocks):
                rows_ref[t, c : c + 1, :] = ref[0, t, row : row + 1, c * LANES : (c + 1) * LANES]
        for u, part in enumerate(to_face([rows_ref[t] for t in range(tracer_count)])):
            out_ref[start + u * blocks : start + (u + 1) * blocks, :] = part
    lane = lax.broadcasted_iota(jnp.int32, (segs, segs), 1)
    row = lax.broadcasted_iota(jnp.int32, (segs, segs), 0)
    source = lane == (row % blocks) * (LANES // SEG) + row // blocks
    target = (dev_ref[...] * segs + permuted(seg_ref[...], blocks)).astype(jnp.float32)
    index = lax.broadcasted_iota(jnp.int32, (segs, LANES), 1)
    order = lax.broadcasted_iota(jnp.int32, (segs, LANES), 0)

    def columns(table):
        return [jnp.sum(jnp.where(source, table[k : k + 1, :], 0.0), axis=1, keepdims=True) for k in range(fanout)]

    targets, weights = columns(target), columns(weight_ref[...])
    own_ref[...] = jnp.zeros_like(own_ref)
    lines = []
    for k, column in enumerate([*targets, *weights]):
        own_ref[:, k : k + 1] = column
    for table in (targets, weights):
        line = 0.0
        for k, column in enumerate(table):
            line = line + jnp.where(index == k * segs + order, column, 0.0)
        lines.append(jnp.sum(line, axis=0, keepdims=True))
    targets, weights = lines
    index = lax.broadcasted_iota(jnp.int32, (TILE, LANES), 0)
    tables = jnp.where(index == 0, targets, jnp.where(index == 1, weights, 0.0))
    out_ref[segs : segs + TILE, :] = tables


def turned(block, stages):
    return sum(bit for k, bit in enumerate(stages) if block >> k & 1)


def merge_kernel(bit, head_ref, sent_ref, received_ref, out_ref):
    segs = (head_ref.shape[0] - TILE) // 2
    size = sent_ref.shape[0] - segs
    out_ref[:size, :] = sent_ref[:size, :]
    out_ref[size : 2 * size, :] = received_ref[:size, :]
    head = head_ref[head_ref.shape[0] - segs :, :]
    passed = received_ref[size:, :]
    out_ref[2 * size :, :] = jnp.where(lax.axis_index("slab") & bit != 0, head, passed)


def middle_kernel(stages, near_ref, far_ref, own_ref, kept_ref, sent_ref):
    _, segs, _ = sent_ref.shape
    stride = segs + TILE
    half = near_ref.shape[0] // stride
    slab_count = 2 * half
    fanout = LANES // segs
    zone, slab = lax.axis_index("zone"), lax.axis_index("slab")
    parts = [(near_ref, i, slab ^ turned(i, stages)) for i in range(half)]
    parts += [(far_ref, i, slab ^ (turned(i, stages) + stages[-1])) for i in range(half)]
    own_face = near_ref[:segs, :]

    def face(ref, i):
        return ref[i * stride : i * stride + segs, :]

    def line(ref, i, k):
        return ref[i * stride + segs + k : i * stride + segs + k + 1, :]

    order = lax.broadcasted_iota(jnp.int32, (segs, LANES), 0)

    def picked(z):
        own = (order + (z * slab_count + slab) * segs).astype(jnp.float32)
        return [
            jnp.where(line(ref, i, 0) == own, line(ref, i, 1), 0.0) for ref, i, _ in parts
        ]

    @pl.when(zone < PIN)
    def _():
        pickers = []
        for _, _, index in parts:
            slots = lax.broadcasted_iota(jnp.int32, (segs, segs), 1) + (zone * slab_count + index) * segs
            slots = slots.astype(jnp.float32)
            picker = jnp.zeros(slots.shape, jnp.float32)
            for k in range(fanout):
                target, weight = own_ref[:, k : k + 1], own_ref[:, fanout + k : fanout + k + 1]
                picker = picker + jnp.where(target == slots, weight, 0.0)
            pickers.append(picker)
        part = jnp.dot(
            jnp.concatenate(pickers, axis=1),
            jnp.concatenate([face(ref, i) for ref, i, _ in parts], axis=0),
            precision=HIGHEST,
            preferred_element_type=jnp.float32,
        )
        sent_ref[0] = part
        sent_ref[1] = jnp.zeros_like(part)
        kept_ref[1] = part
        total = sum(picked(zone))
        kept_ref[0] = -jnp.sum(total, axis=1, keepdims=True) * own_face

    @pl.when(zone == PIN)
    def _():
        faces = jnp.concatenate([face(ref, i) for ref, i, _ in parts for _ in range(fanout)], axis=0)

        def share(z):
            return jnp.dot(
                jnp.concatenate(picked(z), axis=1), faces, precision=HIGHEST, preferred_element_type=jnp.float32
            )

        sent_ref[0] = share(2)
        sent_ref[1] = share(0)
        kept_ref[1] = share(1)
        total = jnp.sum(own_ref[:, fanout : 2 * fanout], axis=1, keepdims=True)
        kept_ref[0] = -total * own_face


def relay_kernel(kept_ref, received_ref, sent_ref):
    zone = lax.axis_index("zone")
    mine = jnp.where(zone == 2, 0.0, kept_ref[1])
    theirs = jnp.where(zone == 1, received_ref[0], jnp.where(zone == 2, received_ref[1], 0.0))
    sent_ref[...] = mine + theirs


def group(low, field, speed, result, diffusivity):
    tracer_count, rows, cols = field.shape
    tiles = GROUP // TILE
    blocks = cols // LANES
    lane = lax.broadcasted_iota(jnp.int32, (TILE, LANES), 1)
    row = lax.broadcasted_iota(jnp.int32, (TILE, LANES), 0)
    is_left, is_right = lane == 0, lane == LANES - 1
    is_top, is_bottom = row == 0, row == TILE - 1
    above = pl.multiple_of(jnp.maximum(low - TILE, 0), TILE)
    below = pl.multiple_of(jnp.minimum(low + GROUP, rows - TILE), TILE)
    has_above = jnp.where(low > 0, 1.0, 0.0)
    has_below = jnp.where(low + GROUP < rows, 1.0, 0.0)

    def cut(block):
        block = jnp.where(block < 0, blocks - 1, jnp.where(block == blocks, 0, block))
        return pl.ds(pl.multiple_of(block * LANES, LANES), LANES)

    def at(tile):
        return pl.ds(pl.multiple_of(low + tile * TILE, TILE), TILE)

    def column(block, carry):
        here = cut(block)
        speeds = []
        for tile in range(tiles):
            a, b = speed[0, at(tile), here], speed[1, at(tile), here]
            a_plus, b_plus = jnp.maximum(a, 0.0), jnp.maximum(b, 0.0)
            a_minus, b_minus = a_plus - a, b_plus - b
            rest = 1.0 - ((a_plus + a_minus) + (b_plus + b_minus))
            speeds.append((a_plus, a_minus, b_plus, b_minus, rest))
        for t in range(tracer_count):
            d = diffusivity[t]
            center = [field[t, pl.ds(above, TILE), here] * has_above]
            center += [field[t, at(tile), here] for tile in range(tiles)]
            center += [field[t, pl.ds(below, TILE), here] * has_below]
            down = [pltpu.roll(x, 1, 0) for x in center[:-1]]
            up = [pltpu.roll(x, TILE - 1, 0) for x in center[1:]]
            for tile in range(tiles):
                a_plus, a_minus, b_plus, b_minus, rest = speeds[tile]
                x = center[tile + 1]
                upper = jnp.where(is_top, down[tile], down[tile + 1])
                lower = jnp.where(is_bottom, up[tile + 1], up[tile])
                left = pltpu.roll(jnp.where(is_right, field[t, at(tile), cut(block - 1)], x), 1, 1)
                right = pltpu.roll(jnp.where(is_left, field[t, at(tile), cut(block + 1)], x), LANES - 1, 1)
                result[t, at(tile), here] = (
                    (rest - 4.0 * d) * x
                    + (a_plus + d) * upper
                    + (a_minus + d) * lower
                    + (b_plus + d) * left
                    + (b_minus + d) * right
                )
        return carry

    lax.fori_loop(0, blocks, column, 0, unroll=UNROLL)


def span(i):
    return pl.ds(pl.multiple_of(i * GROUP, GROUP), GROUP)


def store(result, out_ref, sem, i):
    return pltpu.make_async_copy(result.at[:, span(i), :], out_ref.at[0, :, span(i), :], sem.at[i])


def run_groups(first, last, field, speed, result, diffusivity, out_ref, sem):
    pending = first
    if first > 0:
        pending = first - 1
        store(result, out_ref, sem, pending).start()

    def body(i, carry):
        group(pl.multiple_of(i * GROUP, GROUP), field, speed, result, diffusivity)

        @pl.when(i < last - 1)
        def _():
            store(result, out_ref, sem, i).start()

        return carry

    lax.fori_loop(first, last, body, 0)
    for i in range(pending, last - 1):
        store(result, out_ref, sem, i).wait()


def first_kernel(count, diffusivity_ref, field_ref, speed_ref, result, out_ref, out_sem):
    run_groups(0, count, field_ref.at[0], speed_ref.at[0], result, diffusivity_ref, out_ref, out_sem)


def next_kernel(
    first, last, diffusivity_ref, field, speed, result_in, out_in, result, out_ref, out_sem
):
    del result_in, out_in
    field, speed = field.at[0], speed.at[0]
    run_groups(first, last, field, speed, result, diffusivity_ref, out_ref, out_sem)


def final_kernel(
    first, last, stages, diffusivity_ref, field, speed, result_in, out_in, far_ref, result, out_ref, out_sem
):
    del result_in, out_in
    field, speed = field.at[0], speed.at[0]
    tracer_count, rows, cols = result.shape
    segs = cols // SEG
    slab = lax.axis_index("slab")
    above = jnp.zeros((segs, LANES), jnp.float32)
    stride = segs + TILE
    half = far_ref.shape[0] // stride
    for i in range(half):
        index = slab ^ (turned(i, stages) + stages[-1])
        above = jnp.where(index == slab - 1, far_ref[i * stride : i * stride + segs, :], above)
    below = jnp.where(slab < 2 * half - 1, far_ref[half * stride :, :], 0.0)
    above, below = from_face(above, tracer_count), from_face(below, tracer_count)
    speeds = speed[0, 0:TILE, :][0:1, :]
    up = jnp.maximum(speeds, 0.0)
    for t in range(tracer_count):
        for c in range(cols // LANES):
            here = slice(c * LANES, (c + 1) * LANES)
            result[t, 0:1, here] = result[t, 0:1, here] + (up[:, here] + diffusivity_ref[t]) * above[t][c : c + 1, :]
    top = pltpu.make_async_copy(result.at[:, :TILE, :], out_ref.at[0, :, :TILE, :], out_sem.at[0])
    top.start()
    run_groups(first, last, field, speed, result, diffusivity_ref, out_ref, out_sem)
    speeds = speed[0, rows - TILE : rows, :][TILE - 1 : TILE, :]
    down = jnp.maximum(speeds, 0.0) - speeds
    for t in range(tracer_count):
        for c in range(cols // LANES):
            here = slice(c * LANES, (c + 1) * LANES)
            row = result[t, rows - TILE :, here][TILE - 1 : TILE, :]
            result[t, rows - 1 : rows, here] = row + (down[:, here] + diffusivity_ref[t]) * below[t][c : c + 1, :]
    rest = pl.ds(rows - GROUP, GROUP - TILE)
    tail = pltpu.make_async_copy(result.at[:, rest, :], out_ref.at[0, :, rest, :], out_sem.at[1])
    tail.start()
    top.wait()
    tail.wait()


def last_kernel(kept_ref, first_ref, second_ref, result, partial_ref, out_ref, bottom, sem):
    del partial_ref
    tracer_count, rows, cols = result.shape
    zone = lax.axis_index("zone")
    coupling = kept_ref[0] + jnp.where(zone >= 2, first_ref[0], 0.0) + jnp.where(zone != 2, second_ref[...], 0.0)
    coupling = from_face(COUPLE * coupling, tracer_count)
    bottom[...] = result[:, rows - TILE :, :]
    for t in range(tracer_count):
        for c in range(cols // LANES):
            here = slice(c * LANES, (c + 1) * LANES)
            bottom[t, TILE - 1 : TILE, here] = bottom[t, TILE - 1 : TILE, here] + coupling[t][c : c + 1, :]
    copy = pltpu.make_async_copy(bottom, out_ref.at[0, :, pl.ds(rows - TILE, TILE), :], sem)
    copy.start()
    copy.wait()


def shards(tracers, velocity, diffusivity, owner_dev, owner_seg, intersection):
    zone_count = lax.axis_size("zone")
    slab_count = lax.axis_size("slab")
    _, tracer_count, rows, cols = tracers.shape
    segs = cols // SEG
    f32 = jnp.float32
    small = pltpu.CompilerParams(vmem_limit_bytes=8 * 2**20)
    edge = (1, tracer_count, TILE, cols)
    arguments = tracers, velocity
    tracers, velocity, owner_dev, owner_seg, intersection = (
        pltpu.with_memory_space_constraint(x, pltpu.HBM)
        for x in (tracers, velocity, owner_dev.T, owner_seg.T, intersection.T)
    )
    tables = [pl.BlockSpec(table.shape, lambda i: (0, 0)) for table in (owner_dev, owner_seg, intersection)]
    payload, own = pl.pallas_call(
        pack_kernel,
        grid=(1,),
        out_shape=(
            jax.ShapeDtypeStruct((2 * segs + TILE, LANES), f32),
            jax.ShapeDtypeStruct((segs, LANES), f32),
        ),
        in_specs=[
            pl.BlockSpec(edge, lambda i: (0, 0, 0, 0)),
            pl.BlockSpec(edge, lambda i: (0, 0, rows // TILE - 1, 0)),
            *tables,
        ],
        out_specs=(
            pl.BlockSpec((2 * segs + TILE, LANES), lambda i: (0, 0)),
            pl.BlockSpec((segs, LANES), lambda i: (0, 0)),
        ),
        compiler_params=small,
        scratch_shapes=[pltpu.VMEM((tracer_count, cols // LANES, LANES), f32)],
    )(tracers, tracers, owner_dev, owner_seg, intersection)
    stages = [slab_count >> (k + 1) for k in range(slab_count.bit_length() - 1)]
    groups = rows // GROUP
    field_shape = jax.ShapeDtypeStruct((tracer_count, rows, cols), f32)
    speed_shape = jax.ShapeDtypeStruct((2, rows, cols), f32)
    out_shape = jax.ShapeDtypeStruct(tracers.shape, f32)
    sems = pltpu.SemaphoreType.DMA((groups,))

    def cost(count):
        return pl.CostEstimate(
            flops=20 * tracers.size * count // groups, transcendentals=0, bytes_accessed=20 * rows * cols * count
        )

    def swap(x, axis, bit):
        return lax.ppermute(x, axis, [(i, i ^ bit) for i in range(lax.axis_size(axis))])

    pieces = [p * groups // 8 for p in PIECES]
    field, speed = (pltpu.with_memory_space_constraint(x, pltpu.VMEM) for x in arguments)

    def begin(last, calm):
        return pl.pallas_call(
            functools.partial(first_kernel, last),
            out_shape=(field_shape, out_shape),
            in_specs=[SMEM, VMEM, VMEM],
            out_specs=(VMEM, ANY),
            scratch_shapes=[sems],
            compiler_params=small,
            cost_estimate=cost(last),
        )(calm, field, speed)

    def go_on(first, last, result, out):
        if first == last:
            return result, out
        return pl.pallas_call(
            functools.partial(next_kernel, first, last),
            out_shape=(field_shape, out_shape),
            in_specs=[SMEM, VMEM, VMEM, VMEM, ANY],
            out_specs=(VMEM, ANY),
            scratch_shapes=[sems],
            input_output_aliases={3: 0, 4: 1},
            compiler_params=small,
            cost_estimate=cost(last - first),
        )(diffusivity, field, speed, result, out)

    near, state = payload, None
    for k, bit in enumerate(stages):
        far = swap(near, "slab", bit)
        early = len(stages) - 3
        if k == early:
            state = begin(pieces[0], diffusivity)
        elif k == early + 1:
            state = go_on(pieces[0], pieces[1], *state)
        elif k == early + 2:
            state = go_on(pieces[1], pieces[2], *state)
        if state is not None:
            near, far, *state = lax.optimization_barrier((near, far, *state))
        if k < len(stages) - 1:
            near = pl.pallas_call(
                functools.partial(merge_kernel, stages[k + 1]),
                out_shape=jax.ShapeDtypeStruct((2 * near.shape[0] - segs, LANES), f32),
                in_specs=[VMEM] * 3,
                out_specs=VMEM,
                compiler_params=small,
            )(payload, near, far)
    result, out = state
    kept, sent = pl.pallas_call(
        functools.partial(middle_kernel, stages),
        out_shape=(jax.ShapeDtypeStruct((2, segs, LANES), f32),) * 2,
        in_specs=[VMEM] * 3,
        out_specs=(VMEM, VMEM),
        compiler_params=small,
    )(near, far, own)
    kept, sent, result, out = lax.optimization_barrier((kept, sent, result, out))
    from_x = swap(sent, "zone", 1)
    result, out = go_on(pieces[2], pieces[3], result, out)
    kept, from_x, result, out = lax.optimization_barrier((kept, from_x, result, out))
    relayed = pl.pallas_call(
        relay_kernel,
        out_shape=jax.ShapeDtypeStruct((segs, LANES), f32),
        in_specs=[VMEM] * 2,
        out_specs=VMEM,
        compiler_params=small,
    )(kept, from_x)
    relayed, result, out = lax.optimization_barrier((relayed, result, out))
    from_y = swap(relayed, "zone", 2)
    result, out = pl.pallas_call(
        functools.partial(final_kernel, pieces[3], groups, stages),
        out_shape=(field_shape, out_shape),
        in_specs=[SMEM, VMEM, VMEM, VMEM, ANY, VMEM],
        out_specs=(VMEM, ANY),
        scratch_shapes=[sems],
        input_output_aliases={3: 0, 4: 1},
        compiler_params=small,
        cost_estimate=cost(groups - pieces[3]),
    )(diffusivity, field, speed, result, out, far)
    return pl.pallas_call(
        last_kernel,
        out_shape=out_shape,
        in_specs=[VMEM] * 4 + [ANY],
        out_specs=ANY,
        scratch_shapes=[pltpu.VMEM((tracer_count, TILE, cols), f32), pltpu.SemaphoreType.DMA],
        compiler_params=small,
        input_output_aliases={4: 0},
    )(kept, from_x, from_y, result, out)


def solution(mesh):
    placed = (
        P("zone", None, "slab", None),
        P("zone", None, "slab", None),
        P(),
        P("slab", None),
        P("slab", None),
        P("slab", None),
    )
    return jax.shard_map(
        shards, mesh=mesh, in_specs=placed, out_specs=P("zone", None, "slab", None), check_vma=False
    )
```

time: 118 us -> 26 us (0.22); the launches traced: 116 us -> 25.8 us
  blocking collectives: 46.5 us -> 0 us
  other arithmetic: 29.2 us -> 0 us
  local copies, waits for them, and re-layouts: 22.2 us -> 0.01 us
  Pallas kernels: 0 us -> 13.6 us
  between operations: 13.5 us -> 0.08 us
  starting transfers between devices: 2.85 us -> 8.84 us
  waiting for transfers between devices: 0.02 us -> 3.25 us
  matrix products: 1.48 us -> 0 us
    psum x2 -> x0, blocking collectives: 30.6 us -> none  [the longest x1 16.3 us: from_root(): return lax.psum(block, axis)]
    sub x2 -> x0, other arithmetic: 22 us -> none  [the longest x1 21.2 us: advance(): return center + diffusivity[None, :, None, None] * laplace - transport]
    all_gather x1 -> x0, blocking collectives: 15.9 us -> none  [shards(): zone_faces = lax.all_gather(own_face, 'slab', axis=0, tiled=True)]
    slice x3 -> x0, local copies, waits for them, and re-layouts: 15.9 us -> none  [the longest x2 14.7 us: advance(): left_cells = jnp.roll(center, 1, axis=3)]
    pallas_call x0 -> x10, Pallas kernels: none -> 13.6 us  [the longest x2 5.76 us: go_on(): pl.pallas_call(functools.partial(next_kernel, first, last), out_shape=(fi...]
    ppermute x2 -> x5, starting transfers between devices: 2.85 us -> 8.84 us  [swap(): lax.ppermute(x, axis, [(i, i ^ bit) for i in range(lax.axis_size(axis))])]
    another operation x3 -> x0, other arithmetic: 4.17 us -> none
    ppermute x2 -> x5, waiting for transfers between devices: 0.01 us -> 3.25 us  [swap(): lax.ppermute(x, axis, [(i, i ^ bit) for i in range(lax.axis_size(axis))])]
  transfers between devices with their start and end apart: 3 -> 5, of which waited for: 0 -> 4; matrix products, arithmetic and copies ran while one was open for 36% -> 0% of each run, Pallas kernels for 0% -> 42%
where the time goes in v3:
time: 26 us; the launch traced here: 25.8 us
  Pallas kernels  13.6 us (52%)
  starting transfers between devices  8.84 us (34%)
  waiting for transfers between devices  3.25 us (12%)
    ppermute x5, starting transfers between devices, swap(): lax.ppermute(x, axis, [(i, i ^ bit) for i in range(lax.axis_size(axis))])  8.84 us
    pallas_call x2, Pallas kernels, go_on(): pl.pallas_call(functools.partial(next_kernel, first, last), out_shape=(fi...  5.76 us
    ppermute x5, waiting for transfers between devices, swap(): lax.ppermute(x, axis, [(i, i ^ bit) for i in range(lax.axis_size(axis))])  3.25 us
    pallas_call x1, Pallas kernels, shards(): pl.pallas_call(functools.partial(final_kernel, pieces[3], groups, stages)...  2.74 us
    pallas_call x1, Pallas kernels, begin(): pl.pallas_call(functools.partial(first_kernel, last), out_shape=(field_sh...  2.45 us
    pallas_call x1, Pallas kernels, shards(): pl.pallas_call(pack_kernel, grid=(1,), out_shape=(jax.ShapeDtypeStruct((2...  1.4 us
    pallas_call x1, Pallas kernels, shards(): pl.pallas_call(last_kernel, out_shape=out_shape, in_specs=[VMEM] * 4 + [A...  0.84 us
  transfers between devices with their start and end apart: 5, of which 4 were waited for; matrix products, arithmetic and copies ran while one was open for 0% of the time, Pallas kernels for 42%

profile of v3, /device:TPU:0, one launch (start us, length us, event | category | flops | bytes accessed | tf_op | source)
XLA Modules:
  0.0 25.8 jit_solution(12476847076872481617)
XLA Ops:
  0.0 0.0 copy-start
  0.0 0.0 copy-start.1
  0.0 0.0 copy-start.2
  0.0 1.4 %shard_map.64 = (f32[136,128]{1,0:T(8,128)S(1)}, f32[64,128]{1,0:T(8,128)S(1)}) custom-call(f32[1,4,256,2048]{3,2,1,0:T(8,128)} %field.5, f32[1,4,256,2048]{3,2,1,0:T(8,128)} %field.5, s32[2,64]{1,0:T(2,128)} %bitcast.3, s32[2,64]{1,0:T(2,128)} %bitcast.4, f32[2,64]{1,0:T(2,128)} %bitcast.5), custom_call_target="tpu_custom_call" | custom-call | tf_op jit(solution)/shard_map/pallas_call | solution.py:344
  1.4 4.1 %collective-permute-start = (f32[136,128]{1,0:T(8,128)S(1)}, f32[136,128]{1,0:T(8,128)S(1)}, u32[]{:S(2)}, u32[]{:S(2)}) collective-permute-start(f32[136,128]{1,0:T(8,128)S(1)} %get-tuple-element.43.head_ref.sent_ref), channel_id=1, source_target_pairs={{0,4},{1,5},{2,6},{3,7},{4,0},{5,1},{6,2},{7,3},{8,12},{9,13},{10,... | collective-permute-start | bytes 208904 | tf_op jit(solution)/shard_map/ppermute | solution.py:376
  5.5 0.0 copy-done
  5.5 0.0 copy-done.1
  5.5 0.0 copy-done.2
  5.5 2.4 %shard_map.65 = (f32[4,256,2048]{2,1,0:T(8,128)S(1)}, f32[1,4,256,2048]{3,2,1,0:T(8,128)}) custom-call(f32[4]{0:T(128)S(1)} %copy-done.2, f32[1,4,256,2048]{3,2,1,0:T(8,128)S(1)} %copy-done, f32[1,2,256,2048]{3,2,1,0:T(8,128)S(1)} %copy-done.1), custom_call_target="tpu_custom_call" | custom-call | flops 10485760 | bytes 20971520 | tf_op jit(solution)/shard_map/pallas_call | solution.py:382
  8.0 1.3 %collective-permute-done.received_ref = f32[136,128]{1,0:T(8,128)S(1)} collective-permute-done((f32[136,128]{1,0:T(8,128)S(1)}, f32[136,128]{1,0:T(8,128)S(1)}, u32[]{:S(2)}, u32[]{:S(2)}) %collective-permute-start) | collective-permute-done | bytes 69664 | tf_op jit(solution)/shard_map/ppermute | solution.py:376
  9.3 1.0 %collective-permute-start.1 = (f32[208,128]{1,0:T(8,128)S(1)}, f32[208,128]{1,0:T(8,128)S(1)}, u32[]{:S(2)}, u32[]{:S(2)}) collective-permute-start(f32[208,128]{1,0:T(8,128)S(1)} %shard_map.66.sent_ref), channel_id=1, source_target_pairs={{0,2},{1,3},{2,0},{3,1},{4,6},{5,7},{6,4},{7,5},{8,10},{9,11},{10,... | collective-permute-start | bytes 319496 | tf_op jit(solution)/shard_map/ppermute | solution.py:376
  10.4 3.3 %shard_map.67 = (f32[4,256,2048]{2,1,0:T(8,128)S(1)}, f32[1,4,256,2048]{3,2,1,0:T(8,128)}) custom-call(f32[4]{0:T(128)S(1)} %copy-done.2, f32[1,4,256,2048]{3,2,1,0:T(8,128)S(1)} %copy-done, f32[1,2,256,2048]{3,2,1,0:T(8,128)S(1)} %copy-done.1, f32[4,256,2048]{2,1,0:T(8,128)S(1)} %get-tuple-element.45.result_in, ...), custom_call_target="tpu_custom_call", output_to_operand_aliasing={{0}: (3, {}), {1}: (4, {})} | custom-call | flops 15728640 | bytes 31457280 | tf_op jit(solution)/shard_map/pallas_call | solution.py:395
  13.7 0.4 %collective-permute-done.1.received_ref = f32[208,128]{1,0:T(8,128)S(1)} collective-permute-done((f32[208,128]{1,0:T(8,128)S(1)}, f32[208,128]{1,0:T(8,128)S(1)}, u32[]{:S(2)}, u32[]{:S(2)}) %collective-permute-start.1) | collective-permute-done | bytes 106528 | tf_op jit(solution)/shard_map/ppermute | solution.py:376
  14.1 0.1 collective-permute-start.2
  14.2 1.4 %collective-permute-done.2.far_ref = f32[352,128]{1,0:T(8,128)S(1)} collective-permute-done((f32[352,128]{1,0:T(8,128)S(1)}, f32[352,128]{1,0:T(8,128)S(1)}, u32[]{:S(2)}, u32[]{:S(2)}) %collective-permute-start.2) | collective-permute-done | bytes 180256 | tf_op jit(solution)/shard_map/ppermute | solution.py:376
  15.6 0.4 %shard_map.69 = (f32[2,64,128]{2,1,0:T(8,128)S(1)}, f32[2,64,128]{2,1,0:T(8,128)S(1)}) custom-call(f32[352,128]{1,0:T(8,128)S(1)} %shard_map.68.near_ref, f32[352,128]{1,0:T(8,128)S(1)} %collective-permute-done.2.far_ref, f32[64,128]{1,0:T(8,128)S(1)} %get-tuple-element.55.own_ref), custom_call_target="tpu_custom_call" | custom-call | tf_op jit(solution)/shard_map/pallas_call | solution.py:427
  16.0 1.8 %collective-permute-start.3 = (f32[2,64,128]{2,1,0:T(8,128)S(1)}, f32[2,64,128]{2,1,0:T(8,128)S(1)}, u32[]{:S(2)}, u32[]{:S(2)}) collective-permute-start(f32[2,64,128]{2,1,0:T(8,128)S(1)} %get-tuple-element.61), channel_id=1, source_target_pairs={{0,8},{8,0},{16,24},{24,16},{1,9},{9,1},{17,25},{25,17},{2,10},{10... | collective-permute-start | bytes 196616 | tf_op jit(solution)/shard_map/ppermute | solution.py:376
  17.8 2.4 %shard_map.70 = (f32[4,256,2048]{2,1,0:T(8,128)S(1)}, f32[1,4,256,2048]{3,2,1,0:T(8,128)}) custom-call(f32[4]{0:T(128)S(1)} %copy-done.2, f32[1,4,256,2048]{3,2,1,0:T(8,128)S(1)} %copy-done, f32[1,2,256,2048]{3,2,1,0:T(8,128)S(1)} %copy-done.1, f32[4,256,2048]{2,1,0:T(8,128)S(1)} %get-tuple-element.62.result_in, ...), custom_call_target="tpu_custom_call", output_to_operand_aliasing={{0}: (3, {}), {1}: (4, {})} | custom-call | flops 10485760 | bytes 20971520 | tf_op jit(solution)/shard_map/pallas_call | solution.py:395
  20.2 0.1 collective-permute-done.3.received_ref.first_ref
  20.4 1.9 %collective-permute-start.4 = (f32[64,128]{1,0:T(8,128)S(1)}, f32[64,128]{1,0:T(8,128)S(1)}, u32[]{:S(2)}, u32[]{:S(2)}) collective-permute-start(f32[64,128]{1,0:T(8,128)S(1)} %shard_map.71), channel_id=1, source_target_pairs={{0,16},{8,24},{16,0},{24,8},{1,17},{9,25},{17,1},{25,9},{2,18},{10... | collective-permute-start | bytes 98312 | tf_op jit(solution)/shard_map/ppermute | solution.py:376
  22.2 2.7 %shard_map.72 = (f32[4,256,2048]{2,1,0:T(8,128)S(1)}, f32[1,4,256,2048]{3,2,1,0:T(8,128)}) custom-call(f32[4]{0:T(128)S(1)} %copy-done.2, f32[1,4,256,2048]{3,2,1,0:T(8,128)S(1)} %copy-done, f32[1,2,256,2048]{3,2,1,0:T(8,128)S(1)} %copy-done.1, f32[4,256,2048]{2,1,0:T(8,128)S(1)} %get-tuple-element.71.result_in, ...), custom_call_target="tpu_custom_call", output_to_operand_aliasing={{0}: (3, {}), {1}: (4, {})} | custom-call | flops 5242880 | bytes 10485760 | tf_op jit(solution)/shard_map/pallas_call | solution.py:447
  25.0 0.0 collective-permute-done.4.second_ref
  25.0 0.8 %shard_map.73 = f32[1,4,256,2048]{3,2,1,0:T(8,128)} custom-call(f32[2,64,128]{2,1,0:T(8,128)S(1)} %get-tuple-element.66.kept_ref, f32[2,64,128]{2,1,0:T(8,128)S(1)} %collective-permute-done.3.received_ref.first_ref, f32[64,128]{1,0:T(8,128)S(1)} %collective-permute-done.4.second_ref, ...), custom_call_target="tpu_custom_call", output_to_operand_aliasing={{}: (4, {})} | custom-call | tf_op jit(solution)/shard_map/pallas_call | solution.py:457
  (3 shorter events, 0.0 us)
Async XLA Ops:
  0.0 5.5 %copy-start = (f32[1,4,256,2048]{3,2,1,0:T(8,128)S(1)}, f32[1,4,256,2048]{3,2,1,0:T(8,128)}, u32[]{:S(2)}) copy-start(f32[1,4,256,2048]{3,2,1,0:T(8,128)} %field.5) | copy-start | bytes 25165828
  0.0 5.5 %copy-start.1 = (f32[1,2,256,2048]{3,2,1,0:T(8,128)S(1)}, f32[1,2,256,2048]{3,2,1,0:T(8,128)}, u32[]{:S(2)}) copy-start(f32[1,2,256,2048]{3,2,1,0:T(8,128)} %speed.5) | copy-start | bytes 12582916
  0.0 5.5 %copy-start.2 = (f32[4]{0:T(128)S(1)}, f32[4]{0:T(128)}, u32[]{:S(2)}) copy-start(f32[4]{0:T(128)} %diffusivity_ref.7) | copy-start | bytes 52
  1.4 7.9 %collective-permute-start = (f32[136,128]{1,0:T(8,128)S(1)}, f32[136,128]{1,0:T(8,128)S(1)}, u32[]{:S(2)}, u32[]{:S(2)}) collective-permute-start(f32[136,128]{1,0:T(8,128)S(1)} %get-tuple-element.43.head_ref.sent_ref), channel_id=1, source_target_pairs={{0,4},{1,5},{2,6},{3,7},{4,0},{5,1},{6,2},{7,3},{8,12},{9,13},{10,... | collective-permute-start | bytes 208904 | tf_op jit(solution)/shard_map/ppermute | solution.py:376
  9.3 4.8 %collective-permute-start.1 = (f32[208,128]{1,0:T(8,128)S(1)}, f32[208,128]{1,0:T(8,128)S(1)}, u32[]{:S(2)}, u32[]{:S(2)}) collective-permute-start(f32[208,128]{1,0:T(8,128)S(1)} %shard_map.66.sent_ref), channel_id=1, source_target_pairs={{0,2},{1,3},{2,0},{3,1},{4,6},{5,7},{6,4},{7,5},{8,10},{9,11},{10,... | collective-permute-start | bytes 319496 | tf_op jit(solution)/shard_map/ppermute | solution.py:376
  14.1 1.5 %collective-permute-start.2 = (f32[352,128]{1,0:T(8,128)S(1)}, f32[352,128]{1,0:T(8,128)S(1)}, u32[]{:S(2)}, u32[]{:S(2)}) collective-permute-start(f32[352,128]{1,0:T(8,128)S(1)} %shard_map.68.near_ref), channel_id=1, source_target_pairs={{0,1},{1,0},{2,3},{3,2},{4,5},{5,4},{6,7},{7,6},{8,9},{9,8},{10,11... | collective-permute-start | bytes 540680 | tf_op jit(solution)/shard_map/ppermute | solution.py:376
  16.0 4.3 %collective-permute-start.3 = (f32[2,64,128]{2,1,0:T(8,128)S(1)}, f32[2,64,128]{2,1,0:T(8,128)S(1)}, u32[]{:S(2)}, u32[]{:S(2)}) collective-permute-start(f32[2,64,128]{2,1,0:T(8,128)S(1)} %get-tuple-element.61), channel_id=1, source_target_pairs={{0,8},{8,0},{16,24},{24,16},{1,9},{9,1},{17,25},{25,17},{2,10},{10... | collective-permute-start | bytes 196616 | tf_op jit(solution)/shard_map/ppermute | solution.py:376
  20.4 4.6 %collective-permute-start.4 = (f32[64,128]{1,0:T(8,128)S(1)}, f32[64,128]{1,0:T(8,128)S(1)}, u32[]{:S(2)}, u32[]{:S(2)}) collective-permute-start(f32[64,128]{1,0:T(8,128)S(1)} %shard_map.71), channel_id=1, source_target_pairs={{0,16},{8,24},{16,0},{24,8},{1,17},{9,25},{17,1},{25,9},{2,18},{10... | collective-permute-start | bytes 98312 | tf_op jit(solution)/shard_map/ppermute | solution.py:376

commit v4 on v3

--- a/solution.py
+++ b/solution.py
@@ -304,16 +304,15 @@
             here = slice(c * LANES, (c + 1) * LANES)
             row = result[t, rows - TILE :, here][TILE - 1 : TILE, :]
             result[t, rows - 1 : rows, here] = row + (down[:, here] + diffusivity_ref[t]) * below[t][c : c + 1, :]
-    rest = pl.ds(rows - GROUP, GROUP - TILE)
-    tail = pltpu.make_async_copy(result.at[:, rest, :], out_ref.at[0, :, rest, :], out_sem.at[1])
-    tail.start()
     top.wait()
-    tail.wait()
 
 
 def last_kernel(kept_ref, first_ref, second_ref, result, partial_ref, out_ref, bottom, sem):
     del partial_ref
     tracer_count, rows, cols = result.shape
+    rest = pl.ds(rows - GROUP, GROUP - TILE)
+    tail = pltpu.make_async_copy(result.at[:, rest, :], out_ref.at[0, :, rest, :], sem.at[1])
+    tail.start()
     zone = lax.axis_index("zone")
     coupling = kept_ref[0] + jnp.where(zone >= 2, first_ref[0], 0.0) + jnp.where(zone != 2, second_ref[...], 0.0)
     coupling = from_face(COUPLE * coupling, tracer_count)
@@ -322,9 +321,10 @@
         for c in range(cols // LANES):
             here = slice(c * LANES, (c + 1) * LANES)
             bottom[t, TILE - 1 : TILE, here] = bottom[t, TILE - 1 : TILE, here] + coupling[t][c : c + 1, :]
-    copy = pltpu.make_async_copy(bottom, out_ref.at[0, :, pl.ds(rows - TILE, TILE), :], sem)
+    copy = pltpu.make_async_copy(bottom, out_ref.at[0, :, pl.ds(rows - TILE, TILE), :], sem.at[0])
     copy.start()
     copy.wait()
+    tail.wait()
 
 
 def shards(tracers, velocity, diffusivity, owner_dev, owner_seg, intersection):
@@ -459,7 +459,7 @@
         out_shape=out_shape,
         in_specs=[VMEM] * 4 + [ANY],
         out_specs=ANY,
-        scratch_shapes=[pltpu.VMEM((tracer_count, TILE, cols), f32), pltpu.SemaphoreType.DMA],
+        scratch_shapes=[pltpu.VMEM((tracer_count, TILE, cols), f32), pltpu.SemaphoreType.DMA((2,))],
         compiler_params=small,
         input_output_aliases={4: 0},
     )(kept, from_x, from_y, result, out)

time: 26 us -> 25.5 us (0.981)
  Pallas kernels: 13.6 us -> 12.9 us
    pallas_call x1, Pallas kernels: 2.74 us -> 1.86 us  [shards(): pl.pallas_call(functools.partial(final_kernel, pieces[3], groups, stages)...]
  transfers between devices with their start and end apart: 5 -> 5, of which waited for: 4 -> 5; matrix products, arithmetic and copies ran while one was open for 0% -> 0% of each run, Pallas kernels for 42% -> 40%
where the time goes in v4:
time: 25.5 us; the launch traced here: 25.4 us
  Pallas kernels  12.9 us (51%)
  starting transfers between devices  8.84 us (35%)
  waiting for transfers between devices  3.5 us (14%)
    ppermute x5, starting transfers between devices, swap(): lax.ppermute(x, axis, [(i, i ^ bit) for i in range(lax.axis_size(axis))])  8.84 us
    pallas_call x2, Pallas kernels, go_on(): pl.pallas_call(functools.partial(next_kernel, first, last), out_shape=(fi...  5.76 us
    ppermute x5, waiting for transfers between devices, swap(): lax.ppermute(x, axis, [(i, i ^ bit) for i in range(lax.axis_size(axis))])  3.5 us
    pallas_call x1, Pallas kernels, begin(): pl.pallas_call(functools.partial(first_kernel, last), out_shape=(field_sh...  2.45 us
    pallas_call x1, Pallas kernels, shards(): pl.pallas_call(functools.partial(final_kernel, pieces[3], groups, stages)...  1.86 us
    pallas_call x1, Pallas kernels, shards(): pl.pallas_call(pack_kernel, grid=(1,), out_shape=(jax.ShapeDtypeStruct((2...  1.4 us
    pallas_call x1, Pallas kernels, shards(): pl.pallas_call(last_kernel, out_shape=out_shape, in_specs=[VMEM] * 4 + [A...  1.01 us
  transfers between devices with their start and end apart: 5, of which 5 were waited for; matrix products, arithmetic and copies ran while one was open for 0% of the time, Pallas kernels for 40%

profile of v4, /device:TPU:0, one launch (start us, length us, event | category | flops | bytes accessed | tf_op | source)
XLA Modules:
  0.0 25.4 jit_solution(7429461586078472004)
XLA Ops:
  0.0 0.0 copy-start
  0.0 0.0 copy-start.1
  0.0 0.0 copy-start.2
  0.0 1.4 %shard_map.64 = (f32[136,128]{1,0:T(8,128)S(1)}, f32[64,128]{1,0:T(8,128)S(1)}) custom-call(f32[1,4,256,2048]{3,2,1,0:T(8,128)} %field.5, f32[1,4,256,2048]{3,2,1,0:T(8,128)} %field.5, s32[2,64]{1,0:T(2,128)} %bitcast.3, s32[2,64]{1,0:T(2,128)} %bitcast.4, f32[2,64]{1,0:T(2,128)} %bitcast.5), custom_call_target="tpu_custom_call" | custom-call | tf_op jit(solution)/shard_map/pallas_call | solution.py:344
  1.4 4.1 %collective-permute-start = (f32[136,128]{1,0:T(8,128)S(1)}, f32[136,128]{1,0:T(8,128)S(1)}, u32[]{:S(2)}, u32[]{:S(2)}) collective-permute-start(f32[136,128]{1,0:T(8,128)S(1)} %get-tuple-element.43.head_ref.sent_ref), channel_id=1, source_target_pairs={{0,4},{1,5},{2,6},{3,7},{4,0},{5,1},{6,2},{7,3},{8,12},{9,13},{10,... | collective-permute-start | bytes 208904 | tf_op jit(solution)/shard_map/ppermute | solution.py:376
  5.5 0.0 copy-done
  5.5 0.0 copy-done.1
  5.5 0.0 copy-done.2
  5.5 2.4 %shard_map.65 = (f32[4,256,2048]{2,1,0:T(8,128)S(1)}, f32[1,4,256,2048]{3,2,1,0:T(8,128)}) custom-call(f32[4]{0:T(128)S(1)} %copy-done.2, f32[1,4,256,2048]{3,2,1,0:T(8,128)S(1)} %copy-done, f32[1,2,256,2048]{3,2,1,0:T(8,128)S(1)} %copy-done.1), custom_call_target="tpu_custom_call" | custom-call | flops 10485760 | bytes 20971520 | tf_op jit(solution)/shard_map/pallas_call | solution.py:382
  8.0 1.3 %collective-permute-done.received_ref = f32[136,128]{1,0:T(8,128)S(1)} collective-permute-done((f32[136,128]{1,0:T(8,128)S(1)}, f32[136,128]{1,0:T(8,128)S(1)}, u32[]{:S(2)}, u32[]{:S(2)}) %collective-permute-start) | collective-permute-done | bytes 69664 | tf_op jit(solution)/shard_map/ppermute | solution.py:376
  9.3 1.0 %collective-permute-start.1 = (f32[208,128]{1,0:T(8,128)S(1)}, f32[208,128]{1,0:T(8,128)S(1)}, u32[]{:S(2)}, u32[]{:S(2)}) collective-permute-start(f32[208,128]{1,0:T(8,128)S(1)} %shard_map.66.sent_ref), channel_id=1, source_target_pairs={{0,2},{1,3},{2,0},{3,1},{4,6},{5,7},{6,4},{7,5},{8,10},{9,11},{10,... | collective-permute-start | bytes 319496 | tf_op jit(solution)/shard_map/ppermute | solution.py:376
  10.4 3.3 %shard_map.67 = (f32[4,256,2048]{2,1,0:T(8,128)S(1)}, f32[1,4,256,2048]{3,2,1,0:T(8,128)}) custom-call(f32[4]{0:T(128)S(1)} %copy-done.2, f32[1,4,256,2048]{3,2,1,0:T(8,128)S(1)} %copy-done, f32[1,2,256,2048]{3,2,1,0:T(8,128)S(1)} %copy-done.1, f32[4,256,2048]{2,1,0:T(8,128)S(1)} %get-tuple-element.45.result_in, ...), custom_call_target="tpu_custom_call", output_to_operand_aliasing={{0}: (3, {}), {1}: (4, {})} | custom-call | flops 15728640 | bytes 31457280 | tf_op jit(solution)/shard_map/pallas_call | solution.py:395
  13.7 0.4 %collective-permute-done.1.received_ref = f32[208,128]{1,0:T(8,128)S(1)} collective-permute-done((f32[208,128]{1,0:T(8,128)S(1)}, f32[208,128]{1,0:T(8,128)S(1)}, u32[]{:S(2)}, u32[]{:S(2)}) %collective-permute-start.1) | collective-permute-done | bytes 106528 | tf_op jit(solution)/shard_map/ppermute | solution.py:376
  14.1 0.1 collective-permute-start.2
  14.2 1.4 %collective-permute-done.2.far_ref = f32[352,128]{1,0:T(8,128)S(1)} collective-permute-done((f32[352,128]{1,0:T(8,128)S(1)}, f32[352,128]{1,0:T(8,128)S(1)}, u32[]{:S(2)}, u32[]{:S(2)}) %collective-permute-start.2) | collective-permute-done | bytes 180256 | tf_op jit(solution)/shard_map/ppermute | solution.py:376
  15.6 0.4 %shard_map.69 = (f32[2,64,128]{2,1,0:T(8,128)S(1)}, f32[2,64,128]{2,1,0:T(8,128)S(1)}) custom-call(f32[352,128]{1,0:T(8,128)S(1)} %shard_map.68.near_ref, f32[352,128]{1,0:T(8,128)S(1)} %collective-permute-done.2.far_ref, f32[64,128]{1,0:T(8,128)S(1)} %get-tuple-element.55.own_ref), custom_call_target="tpu_custom_call" | custom-call | tf_op jit(solution)/shard_map/pallas_call | solution.py:427
  16.0 1.8 %collective-permute-start.3 = (f32[2,64,128]{2,1,0:T(8,128)S(1)}, f32[2,64,128]{2,1,0:T(8,128)S(1)}, u32[]{:S(2)}, u32[]{:S(2)}) collective-permute-start(f32[2,64,128]{2,1,0:T(8,128)S(1)} %get-tuple-element.61), channel_id=1, source_target_pairs={{0,8},{8,0},{16,24},{24,16},{1,9},{9,1},{17,25},{25,17},{2,10},{10... | collective-permute-start | bytes 196616 | tf_op jit(solution)/shard_map/ppermute | solution.py:376
  17.8 2.4 %shard_map.70 = (f32[4,256,2048]{2,1,0:T(8,128)S(1)}, f32[1,4,256,2048]{3,2,1,0:T(8,128)}) custom-call(f32[4]{0:T(128)S(1)} %copy-done.2, f32[1,4,256,2048]{3,2,1,0:T(8,128)S(1)} %copy-done, f32[1,2,256,2048]{3,2,1,0:T(8,128)S(1)} %copy-done.1, f32[4,256,2048]{2,1,0:T(8,128)S(1)} %get-tuple-element.62.result_in, ...), custom_call_target="tpu_custom_call", output_to_operand_aliasing={{0}: (3, {}), {1}: (4, {})} | custom-call | flops 10485760 | bytes 20971520 | tf_op jit(solution)/shard_map/pallas_call | solution.py:395
  20.2 0.1 collective-permute-done.3.received_ref.first_ref
  20.4 1.9 %collective-permute-start.4 = (f32[64,128]{1,0:T(8,128)S(1)}, f32[64,128]{1,0:T(8,128)S(1)}, u32[]{:S(2)}, u32[]{:S(2)}) collective-permute-start(f32[64,128]{1,0:T(8,128)S(1)} %shard_map.71), channel_id=1, source_target_pairs={{0,16},{8,24},{16,0},{24,8},{1,17},{9,25},{17,1},{25,9},{2,18},{10... | collective-permute-start | bytes 98312 | tf_op jit(solution)/shard_map/ppermute | solution.py:376
  22.2 1.9 %shard_map.72 = (f32[4,256,2048]{2,1,0:T(8,128)S(1)}, f32[1,4,256,2048]{3,2,1,0:T(8,128)}) custom-call(f32[4]{0:T(128)S(1)} %copy-done.2, f32[1,4,256,2048]{3,2,1,0:T(8,128)S(1)} %copy-done, f32[1,2,256,2048]{3,2,1,0:T(8,128)S(1)} %copy-done.1, f32[4,256,2048]{2,1,0:T(8,128)S(1)} %get-tuple-element.71.result_in, ...), custom_call_target="tpu_custom_call", output_to_operand_aliasing={{0}: (3, {}), {1}: (4, {})} | custom-call | flops 5242880 | bytes 10485760 | tf_op jit(solution)/shard_map/pallas_call | solution.py:447
  24.1 0.2 collective-permute-done.4.second_ref
  24.3 1.0 %shard_map.73 = f32[1,4,256,2048]{3,2,1,0:T(8,128)} custom-call(f32[2,64,128]{2,1,0:T(8,128)S(1)} %get-tuple-element.66.kept_ref, f32[2,64,128]{2,1,0:T(8,128)S(1)} %collective-permute-done.3.received_ref.first_ref, f32[64,128]{1,0:T(8,128)S(1)} %collective-permute-done.4.second_ref, ...), custom_call_target="tpu_custom_call", output_to_operand_aliasing={{}: (4, {})} | custom-call | tf_op jit(solution)/shard_map/pallas_call | solution.py:457
  (3 shorter events, 0.0 us)
Async XLA Ops:
  0.0 5.5 %copy-start = (f32[1,4,256,2048]{3,2,1,0:T(8,128)S(1)}, f32[1,4,256,2048]{3,2,1,0:T(8,128)}, u32[]{:S(2)}) copy-start(f32[1,4,256,2048]{3,2,1,0:T(8,128)} %field.5) | copy-start | bytes 25165828
  0.0 5.5 %copy-start.1 = (f32[1,2,256,2048]{3,2,1,0:T(8,128)S(1)}, f32[1,2,256,2048]{3,2,1,0:T(8,128)}, u32[]{:S(2)}) copy-start(f32[1,2,256,2048]{3,2,1,0:T(8,128)} %speed.5) | copy-start | bytes 12582916
  0.0 5.5 %copy-start.2 = (f32[4]{0:T(128)S(1)}, f32[4]{0:T(128)}, u32[]{:S(2)}) copy-start(f32[4]{0:T(128)} %diffusivity_ref.7) | copy-start | bytes 52
  1.4 7.9 %collective-permute-start = (f32[136,128]{1,0:T(8,128)S(1)}, f32[136,128]{1,0:T(8,128)S(1)}, u32[]{:S(2)}, u32[]{:S(2)}) collective-permute-start(f32[136,128]{1,0:T(8,128)S(1)} %get-tuple-element.43.head_ref.sent_ref), channel_id=1, source_target_pairs={{0,4},{1,5},{2,6},{3,7},{4,0},{5,1},{6,2},{7,3},{8,12},{9,13},{10,... | collective-permute-start | bytes 208904 | tf_op jit(solution)/shard_map/ppermute | solution.py:376
  9.3 4.8 %collective-permute-start.1 = (f32[208,128]{1,0:T(8,128)S(1)}, f32[208,128]{1,0:T(8,128)S(1)}, u32[]{:S(2)}, u32[]{:S(2)}) collective-permute-start(f32[208,128]{1,0:T(8,128)S(1)} %shard_map.66.sent_ref), channel_id=1, source_target_pairs={{0,2},{1,3},{2,0},{3,1},{4,6},{5,7},{6,4},{7,5},{8,10},{9,11},{10,... | collective-permute-start | bytes 319496 | tf_op jit(solution)/shard_map/ppermute | solution.py:376
  14.1 1.5 %collective-permute-start.2 = (f32[352,128]{1,0:T(8,128)S(1)}, f32[352,128]{1,0:T(8,128)S(1)}, u32[]{:S(2)}, u32[]{:S(2)}) collective-permute-start(f32[352,128]{1,0:T(8,128)S(1)} %shard_map.68.near_ref), channel_id=1, source_target_pairs={{0,1},{1,0},{2,3},{3,2},{4,5},{5,4},{6,7},{7,6},{8,9},{9,8},{10,11... | collective-permute-start | bytes 540680 | tf_op jit(solution)/shard_map/ppermute | solution.py:376
  16.0 4.3 %collective-permute-start.3 = (f32[2,64,128]{2,1,0:T(8,128)S(1)}, f32[2,64,128]{2,1,0:T(8,128)S(1)}, u32[]{:S(2)}, u32[]{:S(2)}) collective-permute-start(f32[2,64,128]{2,1,0:T(8,128)S(1)} %get-tuple-element.61), channel_id=1, source_target_pairs={{0,8},{8,0},{16,24},{24,16},{1,9},{9,1},{17,25},{25,17},{2,10},{10... | collective-permute-start | bytes 196616 | tf_op jit(solution)/shard_map/ppermute | solution.py:376
  20.4 4.0 %collective-permute-start.4 = (f32[64,128]{1,0:T(8,128)S(1)}, f32[64,128]{1,0:T(8,128)S(1)}, u32[]{:S(2)}, u32[]{:S(2)}) collective-permute-start(f32[64,128]{1,0:T(8,128)S(1)} %shard_map.71), channel_id=1, source_target_pairs={{0,16},{8,24},{16,0},{24,8},{1,17},{9,25},{17,1},{25,9},{2,18},{10... | collective-permute-start | bytes 98312 | tf_op jit(solution)/shard_map/ppermute | solution.py:376

commit v5 on v4

--- a/solution.py
+++ b/solution.py
@@ -156,16 +156,21 @@
 
     @pl.when(zone == PIN)
     def _():
-        faces = jnp.concatenate([face(ref, i) for ref, i, _ in parts for _ in range(fanout)], axis=0)
-
-        def share(z):
-            return jnp.dot(
-                jnp.concatenate(picked(z), axis=1), faces, precision=HIGHEST, preferred_element_type=jnp.float32
+        faces = jnp.concatenate([face(ref, i) for ref, i, _ in parts], axis=0)
+
+        lane = lax.broadcasted_iota(jnp.int32, (segs, LANES), 1)
+
+        def columns(z):
+            sums = [x + pltpu.roll(x, segs, 1) for x in picked(z)]
+            return jnp.concatenate(
+                [jnp.where(lane < segs, sums[i], sums[i + 1]) for i in range(0, len(sums), 2)], axis=1
             )
 
-        sent_ref[0] = share(2)
-        sent_ref[1] = share(0)
-        kept_ref[1] = share(1)
+        pickers = jnp.concatenate([columns(z) for z in (2, 0, 1)], axis=0)
+        shares = jnp.dot(pickers, faces, precision=HIGHEST, preferred_element_type=jnp.float32)
+        sent_ref[0] = shares[:segs]
+        sent_ref[1] = shares[segs : 2 * segs]
+        kept_ref[1] = shares[2 * segs :]
         total = jnp.sum(own_ref[:, fanout : 2 * fanout], axis=1, keepdims=True)
         kept_ref[0] = -total * own_face
 

time: 25.5 us -> 25.5 us (level)
  no operation moved by 1% of the time
where the time goes in v5:
time: 25.5 us; the launch traced here: 25.4 us
  Pallas kernels  12.9 us (51%)
  starting transfers between devices  8.77 us (34%)
  waiting for transfers between devices  3.57 us (14%)
    ppermute x5, starting transfers between devices, swap(): lax.ppermute(x, axis, [(i, i ^ bit) for i in range(lax.axis_size(axis))])  8.77 us
    pallas_call x2, Pallas kernels, go_on(): pl.pallas_call(functools.partial(next_kernel, first, last), out_shape=(fi...  5.76 us
    ppermute x5, waiting for transfers between devices, swap(): lax.ppermute(x, axis, [(i, i ^ bit) for i in range(lax.axis_size(axis))])  3.57 us
    pallas_call x1, Pallas kernels, begin(): pl.pallas_call(functools.partial(first_kernel, last), out_shape=(field_sh...  2.45 us
    pallas_call x1, Pallas kernels, shards(): pl.pallas_call(functools.partial(final_kernel, pieces[3], groups, stages)...  1.86 us
    pallas_call x1, Pallas kernels, shards(): pl.pallas_call(pack_kernel, grid=(1,), out_shape=(jax.ShapeDtypeStruct((2...  1.4 us
    pallas_call x1, Pallas kernels, shards(): pl.pallas_call(last_kernel, out_shape=out_shape, in_specs=[VMEM] * 4 + [A...  1.01 us
  transfers between devices with their start and end apart: 5, of which 5 were waited for; matrix products, arithmetic and copies ran while one was open for 0% of the time, Pallas kernels for 40%

profile of v5, /device:TPU:0, one launch (start us, length us, event | category | flops | bytes accessed | tf_op | source)
XLA Modules:
  0.0 25.4 jit_solution(2616433088345879981)
XLA Ops:
  0.0 0.0 copy-start
  0.0 0.0 copy-start.1
  0.0 0.0 copy-start.2
  0.0 1.4 %shard_map.64 = (f32[136,128]{1,0:T(8,128)S(1)}, f32[64,128]{1,0:T(8,128)S(1)}) custom-call(f32[1,4,256,2048]{3,2,1,0:T(8,128)} %field.5, f32[1,4,256,2048]{3,2,1,0:T(8,128)} %field.5, s32[2,64]{1,0:T(2,128)} %bitcast.3, s32[2,64]{1,0:T(2,128)} %bitcast.4, f32[2,64]{1,0:T(2,128)} %bitcast.5), custom_call_target="tpu_custom_call" | custom-call | tf_op jit(solution)/shard_map/pallas_call | solution.py:349
  1.4 4.1 %collective-permute-start = (f32[136,128]{1,0:T(8,128)S(1)}, f32[136,128]{1,0:T(8,128)S(1)}, u32[]{:S(2)}, u32[]{:S(2)}) collective-permute-start(f32[136,128]{1,0:T(8,128)S(1)} %get-tuple-element.43.head_ref.sent_ref), channel_id=1, source_target_pairs={{0,4},{1,5},{2,6},{3,7},{4,0},{5,1},{6,2},{7,3},{8,12},{9,13},{10,... | collective-permute-start | bytes 208904 | tf_op jit(solution)/shard_map/ppermute | solution.py:381
  5.5 0.0 copy-done
  5.5 0.0 copy-done.1
  5.5 0.0 copy-done.2
  5.5 2.4 %shard_map.65 = (f32[4,256,2048]{2,1,0:T(8,128)S(1)}, f32[1,4,256,2048]{3,2,1,0:T(8,128)}) custom-call(f32[4]{0:T(128)S(1)} %copy-done.2, f32[1,4,256,2048]{3,2,1,0:T(8,128)S(1)} %copy-done, f32[1,2,256,2048]{3,2,1,0:T(8,128)S(1)} %copy-done.1), custom_call_target="tpu_custom_call" | custom-call | flops 10485760 | bytes 20971520 | tf_op jit(solution)/shard_map/pallas_call | solution.py:387
  8.0 1.3 %collective-permute-done.received_ref = f32[136,128]{1,0:T(8,128)S(1)} collective-permute-done((f32[136,128]{1,0:T(8,128)S(1)}, f32[136,128]{1,0:T(8,128)S(1)}, u32[]{:S(2)}, u32[]{:S(2)}) %collective-permute-start) | collective-permute-done | bytes 69664 | tf_op jit(solution)/shard_map/ppermute | solution.py:381
  9.3 1.0 %collective-permute-start.1 = (f32[208,128]{1,0:T(8,128)S(1)}, f32[208,128]{1,0:T(8,128)S(1)}, u32[]{:S(2)}, u32[]{:S(2)}) collective-permute-start(f32[208,128]{1,0:T(8,128)S(1)} %shard_map.66.sent_ref), channel_id=1, source_target_pairs={{0,2},{1,3},{2,0},{3,1},{4,6},{5,7},{6,4},{7,5},{8,10},{9,11},{10,... | collective-permute-start | bytes 319496 | tf_op jit(solution)/shard_map/ppermute | solution.py:381
  10.4 3.3 %shard_map.67 = (f32[4,256,2048]{2,1,0:T(8,128)S(1)}, f32[1,4,256,2048]{3,2,1,0:T(8,128)}) custom-call(f32[4]{0:T(128)S(1)} %copy-done.2, f32[1,4,256,2048]{3,2,1,0:T(8,128)S(1)} %copy-done, f32[1,2,256,2048]{3,2,1,0:T(8,128)S(1)} %copy-done.1, f32[4,256,2048]{2,1,0:T(8,128)S(1)} %get-tuple-element.45.result_in, ...), custom_call_target="tpu_custom_call", output_to_operand_aliasing={{0}: (3, {}), {1}: (4, {})} | custom-call | flops 15728640 | bytes 31457280 | tf_op jit(solution)/shard_map/pallas_call | solution.py:400
  13.7 0.4 %collective-permute-done.1.received_ref = f32[208,128]{1,0:T(8,128)S(1)} collective-permute-done((f32[208,128]{1,0:T(8,128)S(1)}, f32[208,128]{1,0:T(8,128)S(1)}, u32[]{:S(2)}, u32[]{:S(2)}) %collective-permute-start.1) | collective-permute-done | bytes 106528 | tf_op jit(solution)/shard_map/ppermute | solution.py:381
  14.1 0.1 collective-permute-start.2
  14.2 1.4 %collective-permute-done.2.far_ref = f32[352,128]{1,0:T(8,128)S(1)} collective-permute-done((f32[352,128]{1,0:T(8,128)S(1)}, f32[352,128]{1,0:T(8,128)S(1)}, u32[]{:S(2)}, u32[]{:S(2)}) %collective-permute-start.2) | collective-permute-done | bytes 180256 | tf_op jit(solution)/shard_map/ppermute | solution.py:381
  15.6 0.4 %shard_map.69 = (f32[2,64,128]{2,1,0:T(8,128)S(1)}, f32[2,64,128]{2,1,0:T(8,128)S(1)}) custom-call(f32[352,128]{1,0:T(8,128)S(1)} %shard_map.68.near_ref, f32[352,128]{1,0:T(8,128)S(1)} %collective-permute-done.2.far_ref, f32[64,128]{1,0:T(8,128)S(1)} %get-tuple-element.55.own_ref), custom_call_target="tpu_custom_call" | custom-call | tf_op jit(solution)/shard_map/pallas_call | solution.py:432
  16.0 1.8 %collective-permute-start.3 = (f32[2,64,128]{2,1,0:T(8,128)S(1)}, f32[2,64,128]{2,1,0:T(8,128)S(1)}, u32[]{:S(2)}, u32[]{:S(2)}) collective-permute-start(f32[2,64,128]{2,1,0:T(8,128)S(1)} %get-tuple-element.61), channel_id=1, source_target_pairs={{0,8},{8,0},{16,24},{24,16},{1,9},{9,1},{17,25},{25,17},{2,10},{10... | collective-permute-start | bytes 196616 | tf_op jit(solution)/shard_map/ppermute | solution.py:381
  17.8 2.4 %shard_map.70 = (f32[4,256,2048]{2,1,0:T(8,128)S(1)}, f32[1,4,256,2048]{3,2,1,0:T(8,128)}) custom-call(f32[4]{0:T(128)S(1)} %copy-done.2, f32[1,4,256,2048]{3,2,1,0:T(8,128)S(1)} %copy-done, f32[1,2,256,2048]{3,2,1,0:T(8,128)S(1)} %copy-done.1, f32[4,256,2048]{2,1,0:T(8,128)S(1)} %get-tuple-element.62.result_in, ...), custom_call_target="tpu_custom_call", output_to_operand_aliasing={{0}: (3, {}), {1}: (4, {})} | custom-call | flops 10485760 | bytes 20971520 | tf_op jit(solution)/shard_map/pallas_call | solution.py:400
  20.2 0.1 collective-permute-done.3.received_ref.first_ref
  20.4 1.8 %collective-permute-start.4 = (f32[64,128]{1,0:T(8,128)S(1)}, f32[64,128]{1,0:T(8,128)S(1)}, u32[]{:S(2)}, u32[]{:S(2)}) collective-permute-start(f32[64,128]{1,0:T(8,128)S(1)} %shard_map.71), channel_id=1, source_target_pairs={{0,16},{8,24},{16,0},{24,8},{1,17},{9,25},{17,1},{25,9},{2,18},{10... | collective-permute-start | bytes 98312 | tf_op jit(solution)/shard_map/ppermute | solution.py:381
  22.2 1.9 %shard_map.72 = (f32[4,256,2048]{2,1,0:T(8,128)S(1)}, f32[1,4,256,2048]{3,2,1,0:T(8,128)}) custom-call(f32[4]{0:T(128)S(1)} %copy-done.2, f32[1,4,256,2048]{3,2,1,0:T(8,128)S(1)} %copy-done, f32[1,2,256,2048]{3,2,1,0:T(8,128)S(1)} %copy-done.1, f32[4,256,2048]{2,1,0:T(8,128)S(1)} %get-tuple-element.71.result_in, ...), custom_call_target="tpu_custom_call", output_to_operand_aliasing={{0}: (3, {}), {1}: (4, {})} | custom-call | flops 5242880 | bytes 10485760 | tf_op jit(solution)/shard_map/pallas_call | solution.py:452
  24.0 0.3 %collective-permute-done.4.second_ref = f32[64,128]{1,0:T(8,128)S(1)} collective-permute-done((f32[64,128]{1,0:T(8,128)S(1)}, f32[64,128]{1,0:T(8,128)S(1)}, u32[]{:S(2)}, u32[]{:S(2)}) %collective-permute-start.4) | collective-permute-done | bytes 32800 | tf_op jit(solution)/shard_map/ppermute | solution.py:381
  24.3 1.0 %shard_map.73 = f32[1,4,256,2048]{3,2,1,0:T(8,128)} custom-call(f32[2,64,128]{2,1,0:T(8,128)S(1)} %get-tuple-element.66.kept_ref, f32[2,64,128]{2,1,0:T(8,128)S(1)} %collective-permute-done.3.received_ref.first_ref, f32[64,128]{1,0:T(8,128)S(1)} %collective-permute-done.4.second_ref, ...), custom_call_target="tpu_custom_call", output_to_operand_aliasing={{}: (4, {})} | custom-call | tf_op jit(solution)/shard_map/pallas_call | solution.py:462
  (3 shorter events, 0.0 us)
Async XLA Ops:
  0.0 5.5 %copy-start = (f32[1,4,256,2048]{3,2,1,0:T(8,128)S(1)}, f32[1,4,256,2048]{3,2,1,0:T(8,128)}, u32[]{:S(2)}) copy-start(f32[1,4,256,2048]{3,2,1,0:T(8,128)} %field.5) | copy-start | bytes 25165828
  0.0 5.5 %copy-start.1 = (f32[1,2,256,2048]{3,2,1,0:T(8,128)S(1)}, f32[1,2,256,2048]{3,2,1,0:T(8,128)}, u32[]{:S(2)}) copy-start(f32[1,2,256,2048]{3,2,1,0:T(8,128)} %speed.5) | copy-start | bytes 12582916
  0.0 5.5 %copy-start.2 = (f32[4]{0:T(128)S(1)}, f32[4]{0:T(128)}, u32[]{:S(2)}) copy-start(f32[4]{0:T(128)} %diffusivity_ref.7) | copy-start | bytes 52
  1.4 7.9 %collective-permute-start = (f32[136,128]{1,0:T(8,128)S(1)}, f32[136,128]{1,0:T(8,128)S(1)}, u32[]{:S(2)}, u32[]{:S(2)}) collective-permute-start(f32[136,128]{1,0:T(8,128)S(1)} %get-tuple-element.43.head_ref.sent_ref), channel_id=1, source_target_pairs={{0,4},{1,5},{2,6},{3,7},{4,0},{5,1},{6,2},{7,3},{8,12},{9,13},{10,... | collective-permute-start | bytes 208904 | tf_op jit(solution)/shard_map/ppermute | solution.py:381
  9.3 4.8 %collective-permute-start.1 = (f32[208,128]{1,0:T(8,128)S(1)}, f32[208,128]{1,0:T(8,128)S(1)}, u32[]{:S(2)}, u32[]{:S(2)}) collective-permute-start(f32[208,128]{1,0:T(8,128)S(1)} %shard_map.66.sent_ref), channel_id=1, source_target_pairs={{0,2},{1,3},{2,0},{3,1},{4,6},{5,7},{6,4},{7,5},{8,10},{9,11},{10,... | collective-permute-start | bytes 319496 | tf_op jit(solution)/shard_map/ppermute | solution.py:381
  14.1 1.5 %collective-permute-start.2 = (f32[352,128]{1,0:T(8,128)S(1)}, f32[352,128]{1,0:T(8,128)S(1)}, u32[]{:S(2)}, u32[]{:S(2)}) collective-permute-start(f32[352,128]{1,0:T(8,128)S(1)} %shard_map.68.near_ref), channel_id=1, source_target_pairs={{0,1},{1,0},{2,3},{3,2},{4,5},{5,4},{6,7},{7,6},{8,9},{9,8},{10,11... | collective-permute-start | bytes 540680 | tf_op jit(solution)/shard_map/ppermute | solution.py:381
  16.0 4.3 %collective-permute-start.3 = (f32[2,64,128]{2,1,0:T(8,128)S(1)}, f32[2,64,128]{2,1,0:T(8,128)S(1)}, u32[]{:S(2)}, u32[]{:S(2)}) collective-permute-start(f32[2,64,128]{2,1,0:T(8,128)S(1)} %get-tuple-element.61), channel_id=1, source_target_pairs={{0,8},{8,0},{16,24},{24,16},{1,9},{9,1},{17,25},{25,17},{2,10},{10... | collective-permute-start | bytes 196616 | tf_op jit(solution)/shard_map/ppermute | solution.py:381
  20.4 4.0 %collective-permute-start.4 = (f32[64,128]{1,0:T(8,128)S(1)}, f32[64,128]{1,0:T(8,128)S(1)}, u32[]{:S(2)}, u32[]{:S(2)}) collective-permute-start(f32[64,128]{1,0:T(8,128)S(1)} %shard_map.71), channel_id=1, source_target_pairs={{0,16},{8,24},{16,0},{24,8},{1,17},{9,25},{17,1},{25,9},{2,18},{10... | collective-permute-start | bytes 98312 | tf_op jit(solution)/shard_map/ppermute | solution.py:381
